TPU v7x, 256 devices: a whole 4x4x8 slice. The times are simulated.
256 devices in a mesh: dom: 64 (over z, y, core), edge: 4 (over x).
Axes of the slice: x: 4, y: 4, z: 8, core: 2. Of those that a mesh axis runs over, the one named last changes fastest.
Arguments:
- fine_nodes: bfloat16 [524288, 128], P('dom'), may hold values from -6 to 6
- fine_edges: bfloat16 [1048576, 128], P(('dom', 'edge')), may hold values from -6 to 6
- fine_senders: int32 [1048576], P(('dom', 'edge')), may hold values from 0 to 12287, as said below
- fine_receivers: int32 [1048576], P(('dom', 'edge')), may hold values from 0 to 8191
- fine_halo: int32 [64, 64, 64], P('dom'), may hold values from 0 to 8191
- coarse_edges: bfloat16 [262144, 128], P(('dom', 'edge')), may hold values from -6 to 6
- coarse_senders: int32 [262144], P(('dom', 'edge')), may hold values from 0 to 4095, as said below
- coarse_receivers: int32 [262144], P(('dom', 'edge')), may hold values from 0 to 2047
- coarse_halo: int32 [64, 64, 32], P('dom'), may hold values from 0 to 2047
- pool_send: int32 [64, 64, 192], P('dom'), may hold values from 0 to 8191, as said below
- pool_dest: int32 [64, 64, 192], P('dom'), may hold values from 0 to 2048, as said below
- unpool_slot: int32 [524288], P('dom'), may hold values from 0 to 12287, as said below
- edge_in_weight: bfloat16 [2, 384, 128], replicated, may hold values from -0.3125 to 0.3125
- edge_out_weight: bfloat16 [2, 128, 128], replicated, may hold values from -0.5 to 0.5
- node_in_weight: bfloat16 [2, 256, 128], replicated, may hold values from -0.375 to 0.375
- node_out_weight: bfloat16 [2, 128, 128], replicated, may hold values from -0.5 to 0.5
- edge_gain: float32 [2, 128], replicated, may hold values from 0.5 to 1.5
- node_gain: float32 [2, 128], replicated, may hold values from 0.5 to 1.5
Outputs:
- fine_out: bfloat16 [524288, 128], P('dom')
- coarse_out: bfloat16 [131072, 128], P('dom')
Inputs may be any that keep to these rules, and one draw needn't show every extreme that they name: `fine_senders`: an entry below 8192 is a row of the edge's own partition; an entry 8192 + d * 64 + s names slot s of fine_halo[d, p] for the edge's partition p. `coarse_senders`: an entry below 2048 is a row of the edge's own coarse partition; an entry 2048 + d * 32 + s names slot s of coarse_halo[d, p]. pool_send[d, p, s] is a row of partition d. For each pair (d, p) the slots that carry data come first and number at most 192; in every draw some p receives 192 from every d. Every row of partition d is carried exactly once over all p and s; empty slots hold 0. pool_dest[p, d, s] is 2048 exactly where slot s of pool_send[d, p] is empty, else a row of coarse partition p. `unpool_slot`: row r of partition d holds p * 192 + s for the one carrying slot with pool_send[d, p, s] = r.
All inputs are finite; a program needn't handle non-finite values.
Results may differ from a plain program's by a relative error of at most 0.0068.
Values may be sent and summed in bfloat16 or wider, within the bound.
A program may use at most 64 MiB of HBM per device.

v0:
```python
import functools

import jax
import jax.numpy as jnp
from jax import lax
from jax.experimental import pallas as pl
from jax.experimental.pallas import tpu as pltpu
from jax.sharding import PartitionSpec as P

F32, BF16 = jnp.float32, jnp.bfloat16
VMEM = pl.BlockSpec(memory_space=pltpu.VMEM)
SMEM = pl.BlockSpec(memory_space=pltpu.SMEM)
LANES = 128


def silu(v):
    return v / (1.0 + jnp.exp(-v))


def normed(v, gain):
    center = v - jnp.mean(v, axis=-1, keepdims=True)
    spread = jnp.mean(center * center, axis=-1, keepdims=True)
    return center * lax.rsqrt(spread + 1e-05) * gain


def dot(a, b):
    return jnp.dot(a, b, preferred_element_type=F32)


def node_mlp(rows, summed, w_in, w_out, gain):
    pre = dot(rows, w_in[0:LANES, :]) + dot(summed.astype(BF16), w_in[LANES : 2 * LANES, :])
    hidden = silu(pre).astype(BF16)
    return (rows.astype(F32) + normed(dot(hidden, w_out), gain)).astype(BF16)


def row_loop(total, step, body):
    def run(i, carry):
        body(pl.multiple_of(i * step, step))
        return carry

    lax.fori_loop(0, total // step, run, 0)


def widen(src, dst, step=512):
    def body(at):
        dst[pl.ds(at, step), :] = src[pl.ds(at, step), :].astype(F32)

    row_loop(src.shape[0], step, body)


def gather_rows(index, table, dst, count, unroll=16):
    def body(at):
        for j in range(unroll):
            dst[pl.ds(at + j, 1), :] = table[pl.ds(index[at + j], 1), :]

    row_loop(count, unroll, body)


def clear_all(accs, step=512):
    def body(at):
        for acc in accs:
            acc[pl.ds(at, step), :] = jnp.zeros((step, LANES), F32)

    row_loop(accs[0].shape[0] // step * step, step, body)


def add_rows(where, values, count, accs, unroll=16):
    def body(at):
        for j in range(0, unroll, 2):
            acc = accs[(j // 2) % len(accs)]
            first, second = where(at + j), where(at + j + 1)
            value = acc[pl.ds(first, 1), :] + values[pl.ds(at + j, 1), :]
            other = acc[pl.ds(second, 1), :]
            other = jnp.where(first == second, value, other) + values[pl.ds(at + j + 1, 1), :]
            acc[pl.ds(first, 1), :] = value
            acc[pl.ds(second, 1), :] = other

    row_loop(count, unroll, body)


def sum_accs(accs, out, step=512):
    def body(at):
        value = accs[0][pl.ds(at, step), :]
        for acc in accs[1:]:
            value = value + acc[pl.ds(at, step), :]
        out[pl.ds(at, step), :] = value.astype(BF16)

    row_loop(out.shape[0], step, body)


def premultiply(rows, weight, dst, base=0, step=512):
    def body(at):
        dst[pl.ds(pl.multiple_of(base + at, step), step), :] = dot(rows[pl.ds(at, step), :], weight)

    row_loop(rows.shape[0], step, body)


def edge_mlp(msg, w_out, gain, out, step=512):
    def body(at):
        hidden = silu(msg[pl.ds(at, step), :]).astype(BF16)
        out[pl.ds(at, step), :] = normed(dot(hidden, w_out), gain)

    row_loop(msg.shape[0], step, body)


def coarse_edge_kernel(senders, receivers, nodes, ghosts, edges, w_in, w_out, gain, out, table_s, table_r, msg, *accs):
    rows, count = nodes.shape[0], edges.shape[0]
    w = w_in[1]
    premultiply(nodes, w[0:LANES, :], table_s)
    premultiply(nodes, w[LANES : 2 * LANES, :], table_r)
    premultiply(ghosts, w[0:LANES, :], table_s, rows)
    premultiply(edges, w[2 * LANES :, :], msg)
    clear_all(accs)

    def gather(at):
        for j in range(32):
            msg[pl.ds(at + j, 1), :] = msg[pl.ds(at + j, 1), :] + (
                table_s[pl.ds(senders[at + j], 1), :] + table_r[pl.ds(receivers[at + j], 1), :]
            )

    row_loop(count, 32, gather)
    edge_mlp(msg, w_out[1], gain[1:2, :], msg)
    add_rows(lambda j: receivers[j], msg, count, accs)
    sum_accs(accs, out)


def coarse_edge_stage(senders, receivers, nodes, ghosts, edges, w_in, w_out, gain):
    rows, far, count = nodes.shape[0], ghosts.shape[0], edges.shape[0]
    return pl.pallas_call(
        coarse_edge_kernel,
        out_shape=jax.ShapeDtypeStruct((rows, LANES), BF16),
        in_specs=[SMEM] * 2 + [VMEM] * 6,
        out_specs=VMEM,
        scratch_shapes=[
            pltpu.VMEM((rows + far, LANES), F32),
            pltpu.VMEM((rows, LANES), F32),
            pltpu.VMEM((count, LANES), F32),
        ]
        + [pltpu.VMEM((rows, LANES), F32)] * 2,
        name="coarse_edge_stage",
    )(senders, receivers, nodes, ghosts, edges, w_in, w_out, gain)


def sum_kernel(receivers, place, msg, out, *accs):
    clear_all(accs)
    add_rows(lambda j: place[receivers[j]], msg, msg.shape[0], accs)
    sum_accs(accs, out)


def sum_stage(receivers, place, msg, slots):
    return pl.pallas_call(
        sum_kernel,
        out_shape=jax.ShapeDtypeStruct((slots, LANES), BF16),
        in_specs=[SMEM, SMEM, VMEM],
        out_specs=VMEM,
        scratch_shapes=[pltpu.VMEM((slots, LANES), F32)] * 2,
        name="sum_stage",
    )(receivers, place, msg)


def pool_kernel(dest, arrived, out, wide, *accs):
    clear_all(accs)
    widen(arrived, wide)
    add_rows(lambda j: dest[j], wide, arrived.shape[0], accs)
    sum_accs(accs, out)


def pool_stage(dest, arrived, rows):
    return pl.pallas_call(
        pool_kernel,
        out_shape=jax.ShapeDtypeStruct((rows, LANES), BF16),
        in_specs=[SMEM, VMEM],
        out_specs=VMEM,
        scratch_shapes=[pltpu.VMEM(arrived.shape, F32)] + [pltpu.VMEM((rows + 8, LANES), F32)] * 2,
        name="pool_stage",
    )(dest, arrived)


def final_kernel(index, table, out, wide, rows):
    widen(table, wide)
    gather_rows(index, wide, rows, out.shape[0], 64)

    def pack(at):
        out[pl.ds(at, 512), :] = rows[pl.ds(at, 512), :].astype(BF16)

    row_loop(out.shape[0], 512, pack)


def final_stage(index, table):
    count = index.shape[0]
    return pl.pallas_call(
        final_kernel,
        out_shape=jax.ShapeDtypeStruct((count, LANES), BF16),
        in_specs=[SMEM, VMEM],
        out_specs=VMEM,
        scratch_shapes=[pltpu.VMEM(table.shape, F32), pltpu.VMEM((count, LANES), F32)],
        name="final_stage",
    )(index, table)


class Net:
    def __init__(self, doms, groups):
        self.doms, self.groups, self.per = doms, groups, doms // groups
        self.me = lax.axis_index("dom")
        self.e = lax.axis_index("edge")
        self.group = self.me // self.per
        self.local = lax.rem(self.me, self.per)
        self.right = lax.rem(self.e + 1, 4)
        self.left = lax.rem(self.e + 3, 4)
        self.opp = lax.rem(self.e + 2, 4)

    def greet(self):
        sem = pltpu.get_barrier_semaphore()
        pl.semaphore_signal(sem, 1, device_id={"edge": self.right})
        pl.semaphore_signal(sem, 1, device_id={"edge": self.left})

        def signal(k, carry):
            pl.semaphore_signal(sem, 1, device_id={"dom": lax.rem(self.me + k, self.doms)})
            return carry

        lax.fori_loop(1, self.doms, signal, 0)

    def meet(self):
        pl.semaphore_wait(pltpu.get_barrier_semaphore(), self.doms + 1)

    def offset(self, t):
        odd = lax.rem(t, 2)
        return odd * ((t + 1) // 2) + (1 - odd) * lax.rem(self.groups - t // 2, self.groups)

    def ahead(self, t):
        return lax.rem(self.group + self.offset(t), self.groups) * self.per

    def behind(self, t):
        return lax.rem(self.group + self.groups - self.offset(t), self.groups) * self.per


class Exchange:
    def __init__(self, net, first, source, target, landed, sems):
        self.net, self.first, self.source, self.target, self.landed = net, first, source, target, landed
        self.send_sem, self.recv_sem, self.own_sem = sems

    def copy(self, t, i):
        net = self.net
        local = lax.rem(net.local + i, net.per)
        peer = self.first(t) + local
        return pltpu.make_async_remote_copy(
            src_ref=self.source(t, peer),
            dst_ref=self.target(t),
            send_sem=self.send_sem.at[t * net.per + local],
            recv_sem=self.recv_sem.at[t * net.per + net.local],
            device_id={"dom": peer},
        )

    def own(self):
        return pltpu.make_async_copy(self.source(0, self.net.me), self.target(0), self.own_sem)

    def each(self, t, body):
        def run(i, carry):
            body(i)
            return carry

        lax.fori_loop(jnp.where(t == 0, 1, 0), self.net.per, run, 0)

    def send(self, t):
        self.each(t, lambda i: self.copy(t, i).start())

    def receive(self, t):
        net = self.net

        def wait(i):
            local = lax.rem(net.local + i, net.per)
            pltpu.make_async_remote_copy(
                src_ref=self.landed(t, local),
                dst_ref=self.landed(t, local),
                send_sem=self.send_sem.at[t * net.per + local],
                recv_sem=self.recv_sem.at[t * net.per + local],
                device_id={"dom": self.first(t) + local},
            ).wait_recv()

        self.each(t, wait)

    def loop(self, body):
        def run(t, carry):
            body(t)
            return carry

        lax.fori_loop(0, self.net.groups, run, 0)

    def finish(self):
        self.own().wait()
        self.loop(lambda t: self.each(t, lambda i: self.copy(t, i).wait_send()))


def exchange_sems(doms):
    return [pltpu.SemaphoreType.DMA((doms,)), pltpu.SemaphoreType.DMA((doms,)), pltpu.SemaphoreType.DMA]


def edge_copy(src, dst, sems, which, slot, to):
    return pltpu.make_async_remote_copy(
        src_ref=src,
        dst_ref=dst,
        send_sem=sems[0].at[which, slot],
        recv_sem=sems[1].at[which, slot],
        device_id={"edge": to},
    )


class Relay:
    def __init__(self, net, out, sems, pieces):
        self.net, self.out, self.sems, self.pieces = net, out, sems, pieces
        self.size = out.shape[1] // pieces

    def copy(self, which, owner, s, half, to):
        if half is None:
            at = pl.ds(s * self.size, self.size)
        else:
            at = pl.ds(s * self.size + half * (self.size // 2), self.size // 2)
        piece = self.out.at[owner, at]
        return edge_copy(piece, piece, self.sems, which, s, to)

    def first(self, s):
        n = self.net
        self.copy(0, n.e, s, None, n.right).start()
        self.copy(1, n.e, s, None, n.left).start()

    def second(self, s):
        n = self.net
        self.copy(0, n.left, s, None, n.right).wait_recv()
        self.copy(2, n.left, s, 0, n.right).start()
        self.copy(1, n.right, s, None, n.left).wait_recv()
        self.copy(3, n.right, s, 1, n.left).start()

    def finish(self, s):
        n = self.net
        self.copy(2, n.opp, s, 0, n.right).wait_recv()
        self.copy(3, n.opp, s, 1, n.left).wait_recv()
        self.copy(0, n.e, s, None, n.right).wait_send()
        self.copy(1, n.e, s, None, n.left).wait_send()
        self.copy(2, n.left, s, 0, n.right).wait_send()
        self.copy(3, n.right, s, 1, n.left).wait_send()

    def run(self, ready=lambda s: None, work=lambda s: None):
        for s in range(self.pieces):
            ready(s)
            self.first(s)
            if s:
                self.second(s - 1)
            work(s)
        self.second(self.pieces - 1)
        for s in range(self.pieces):
            self.finish(s)


def relay_sems(pieces):
    return [pltpu.SemaphoreType.DMA((4, pieces)), pltpu.SemaphoreType.DMA((4, pieces))]


class Reduce:
    def __init__(self, net, part, hop, passed, near, sems, chunks):
        self.net, self.part, self.hop, self.passed, self.near = net, part, hop, passed, near
        self.sems, self.chunks = sems, chunks
        self.half = part.shape[1] // 2
        self.size = self.half // chunks

    def a(self, c):
        return pl.ds(pl.multiple_of(c * self.size, self.size), self.size)

    def b(self, c):
        return pl.ds(pl.multiple_of(self.half + c * self.size, self.size), self.size)

    def hop_right(self, c):
        return edge_copy(self.part.at[self.net.opp, self.a(c)], self.hop.at[0, self.a(c)], self.sems, 0, c, self.net.right)

    def hop_left(self, c):
        return edge_copy(self.part.at[self.net.opp, self.b(c)], self.hop.at[1, self.a(c)], self.sems, 1, c, self.net.left)

    def raw_right(self, c):
        return edge_copy(self.part.at[self.net.right, self.b(c)], self.near.at[0, self.b(c)], self.sems, 2, c, self.net.right)

    def raw_left(self, c):
        return edge_copy(self.part.at[self.net.left, self.a(c)], self.near.at[1, self.a(c)], self.sems, 3, c, self.net.left)

    def sum_right(self, c):
        return edge_copy(self.passed.at[0, self.a(c)], self.near.at[0, self.a(c)], self.sems, 4, c, self.net.right)

    def sum_left(self, c):
        return edge_copy(self.passed.at[1, self.a(c)], self.near.at[1, self.b(c)], self.sems, 5, c, self.net.left)

    def loop(self, body):
        def run(c, carry):
            body(c)
            return carry

        lax.fori_loop(0, self.chunks, run, 0)

    def start(self, c):
        self.hop_right(c).start()
        self.hop_left(c).start()
        self.raw_right(c).start()
        self.raw_left(c).start()

    def through(self, c):
        net = self.net
        self.hop_right(c).wait_recv()
        self.passed[0, self.a(c)] = (
            self.hop[0, self.a(c)].astype(F32) + self.part[net.right, self.a(c)].astype(F32)
        ).astype(BF16)
        self.hop_left(c).wait_recv()
        self.passed[1, self.a(c)] = (
            self.hop[1, self.a(c)].astype(F32) + self.part[net.left, self.b(c)].astype(F32)
        ).astype(BF16)
        self.hop_right(c).wait_send()
        self.hop_left(c).wait_send()
        self.sum_right(c).start()
        self.sum_left(c).start()

    def finish(self, c):
        for copy in (self.raw_right(c), self.raw_left(c), self.sum_right(c), self.sum_left(c)):
            copy.wait()

    def run(self, use=lambda c: None):
        self.start(0)
        for c in range(self.chunks):
            if c + 1 < self.chunks:
                self.start(c + 1)
            self.through(c)
            if c:
                self.finish(c - 1)
                use(c - 1)
        self.finish(self.chunks - 1)
        use(self.chunks - 1)

    def value(self, rows):
        return (
            self.part[self.net.e, rows].astype(F32)
            + self.near[0, rows].astype(F32)
            + self.near[1, rows].astype(F32)
        )


def reduce_scratch(rows, chunks):
    return [
        pltpu.VMEM((2, rows // 2, LANES), BF16),
        pltpu.VMEM((2, rows // 2, LANES), BF16),
        pltpu.VMEM((2, rows, LANES), BF16),
        pltpu.SemaphoreType.DMA((6, chunks)),
        pltpu.SemaphoreType.DMA((6, chunks)),
    ]


def gather_blocks(index, base, table, rows, dst, blocks):
    size = dst.shape[1]

    def body(i, carry):
        k = blocks[0] + i
        start, at = base(k), pl.multiple_of(k * size, size)
        for j in range(size):
            rows[pl.ds(at + j, 1), :] = table[pl.ds(index[start + j], 1), :]
        dst[k] = rows[pl.ds(at, size), :].astype(BF16)
        return carry

    lax.fori_loop(0, blocks[1], body, 0)


def message_kernel(
    groups, pieces, halo, pool_send, senders, receivers, nodes, edges, w_in, w_out, gain,
    out, own_nodes, ghosts, wide, rows, send, table_s, table_r, msg, s0, s1, s2, r0, r1,
):
    doms, size, own_size = ghosts.shape[1], ghosts.shape[2], own_nodes.shape[1]
    count, near = edges.shape[0], nodes.shape[0]
    net = Net(doms, groups)
    net.greet()
    widen(nodes, wide)
    gather_blocks(halo, lambda k: k * (4 * size) + net.e * size, wide, rows, send, (0, doms))
    net.meet()
    land = ghosts.at[net.e]
    exchange = Exchange(
        net, net.ahead,
        lambda t, peer: send.at[peer],
        lambda t: land.at[t * net.per + net.local],
        lambda t, l: land.at[t * net.per + l],
        (s0, s1, s2),
    )
    exchange.own().start()
    exchange.loop(exchange.send)
    w = w_in[0]
    premultiply(nodes, w[LANES : 2 * LANES, :], table_r)
    premultiply(edges, w[2 * LANES :, :], msg)

    def gather_near(at):
        for j in range(32):
            msg[pl.ds(at + j, 1), :] = msg[pl.ds(at + j, 1), :] + table_r[pl.ds(receivers[at + j], 1), :]

    row_loop(count, 32, gather_near)
    each = groups // pieces

    def ready(s):
        def run(t, carry):
            exchange.receive(t)
            return carry

        lax.fori_loop(s * each, (s + 1) * each, run, 0)
        if s == 0:
            exchange.own().wait()

    def base(k):
        p = net.behind(k // net.per) + lax.rem(k, net.per)
        return p * (4 * own_size) + net.e * own_size

    def work(s):
        gather_blocks(pool_send, base, wide, rows, own_nodes, (s * (doms // pieces), doms // pieces))
        if s == pieces - 1:
            premultiply(nodes, w[0:LANES, :], table_s)

    Relay(net, ghosts, (r0, r1), pieces).run(ready, work)
    for owner in range(4):
        block = ghosts[owner].reshape(doms * size, LANES)
        table_s[pl.ds(near + owner * doms * size, doms * size), :] = dot(block, w[0:LANES, :])

    def gather_far(at):
        for j in range(32):
            msg[pl.ds(at + j, 1), :] = msg[pl.ds(at + j, 1), :] + table_s[pl.ds(senders[at + j], 1), :]

    row_loop(count, 32, gather_far)
    edge_mlp(msg, w_out[0], gain[0:1, :], out)
    exchange.loop(lambda t: exchange.each(t, lambda i: exchange.copy(t, i).wait_send()))


def comm_params(collective_id):
    return pltpu.CompilerParams(collective_id=collective_id, has_side_effects=True)


def message_stage(doms, groups, halo, pool_send, senders, receivers, nodes, edges, w_in, w_out, gain, pieces=2):
    size, own_size = halo.shape[0] // doms // 4, pool_send.shape[0] // doms // 4
    near, count = nodes.shape[0], edges.shape[0]
    return pl.pallas_call(
        functools.partial(message_kernel, groups, pieces),
        out_shape=(
            jax.ShapeDtypeStruct((count, LANES), F32),
            jax.ShapeDtypeStruct((doms, own_size, LANES), BF16),
        ),
        in_specs=[SMEM] * 4 + [VMEM] * 5,
        out_specs=(VMEM, VMEM),
        scratch_shapes=[
            pltpu.VMEM((4, doms, size, LANES), BF16),
            pltpu.VMEM(nodes.shape, F32),
            pltpu.VMEM((doms * own_size, LANES), F32),
            pltpu.VMEM((doms, size, LANES), BF16),
            pltpu.VMEM((near + 4 * doms * size, LANES), F32),
            pltpu.VMEM((near, LANES), F32),
            pltpu.VMEM((count, LANES), F32),
        ]
        + exchange_sems(doms)
        + relay_sems(pieces),
        compiler_params=comm_params(0),
        name="message_stage",
    )(halo, pool_send, senders, receivers, nodes, edges, w_in, w_out, gain)


def fine_kernel(groups, part, nodes, w_in, w_out, gain, mid, arrived, hop, passed, near, c0, c1, s0, s1, s2):
    doms, size = mid.shape[0], mid.shape[1]
    net = Net(doms, groups)
    net.greet()
    net.meet()
    reduce = Reduce(net, part, hop, passed, near, (c0, c1), groups // 2)
    exchange = Exchange(
        net, net.behind,
        lambda t, peer: mid.at[t * net.per + lax.rem(peer, net.per)],
        lambda t: arrived.at[net.me],
        lambda t, l: arrived.at[net.ahead(t) + l],
        (s0, s1, s2),
    )
    span = net.per * size

    def use(c):
        units = (c, groups // 2 + c)
        for u in units:
            own = nodes[u * net.per : (u + 1) * net.per].reshape(span, LANES)
            result = node_mlp(own, reduce.value(pl.ds(u * span, span)), w_in[0], w_out[0], gain[0:1, :])
            mid[u * net.per : (u + 1) * net.per] = result.reshape(net.per, size, LANES)
        if c == 0:
            exchange.own().start()
        for u in units:
            exchange.send(u)

    reduce.run(use)
    exchange.loop(exchange.receive)
    exchange.finish()


def fine_stage(groups, part, nodes, w_in, w_out, gain):
    return pl.pallas_call(
        functools.partial(fine_kernel, groups),
        out_shape=(jax.ShapeDtypeStruct(nodes.shape, BF16), jax.ShapeDtypeStruct(nodes.shape, BF16)),
        in_specs=[VMEM] * 5,
        out_specs=(VMEM, VMEM),
        scratch_shapes=reduce_scratch(part.shape[1], groups // 2) + exchange_sems(nodes.shape[0]),
        compiler_params=comm_params(1),
        name="fine_stage",
    )(part, nodes, w_in, w_out, gain)


def coarse_border_kernel(
    groups, chunks, halo, part, count, full, out, wide, rows, send, hop, passed, near, c0, c1, g0, g1, s0, s1, s2, r0, r1
):
    doms, size = out.shape[1], out.shape[2]
    net = Net(doms, groups)
    net.greet()
    net.meet()
    reduce = Reduce(net, part, hop, passed, near, (c0, c1), chunks)
    reduce.run()
    quarter = part.shape[1]
    full[net.e] = (reduce.value(pl.ds(0, quarter)) / count[...]).astype(BF16)
    Relay(net, full, (g0, g1), 1).run()
    for q in range(4):
        wide[pl.ds(q * quarter, quarter), :] = full[q].astype(F32)
    gather_blocks(halo, lambda k: k * (4 * size) + net.e * size, wide, rows, send, (0, doms))
    land = out.at[net.e]
    exchange = Exchange(
        net, net.ahead,
        lambda t, peer: send.at[peer],
        lambda t: land.at[t * net.per + net.local],
        lambda t, l: land.at[t * net.per + l],
        (s0, s1, s2),
    )
    exchange.own().start()
    exchange.loop(exchange.send)
    exchange.loop(exchange.receive)
    exchange.finish()
    Relay(net, out, (r0, r1), 1).run()


def coarse_border_stage(doms, groups, halo, part, count, chunks=2):
    quarter, size = part.shape[1], halo.shape[0] // doms // 4
    return pl.pallas_call(
        functools.partial(coarse_border_kernel, groups, chunks),
        out_shape=(
            jax.ShapeDtypeStruct(part.shape, BF16),
            jax.ShapeDtypeStruct((4, doms, size, LANES), BF16),
        ),
        in_specs=[SMEM, VMEM, VMEM],
        out_specs=(VMEM, VMEM),
        scratch_shapes=[
            pltpu.VMEM((4 * quarter, LANES), F32),
            pltpu.VMEM((doms * size, LANES), F32),
            pltpu.VMEM((doms, size, LANES), BF16),
        ]
        + reduce_scratch(quarter, chunks)
        + relay_sems(1)
        + exchange_sems(doms)
        + relay_sems(1),
        compiler_params=comm_params(2),
        name="coarse_border_stage",
    )(halo, part, count)


def unpool_kernel(
    groups, chunks, pieces, index, part, nodes, mid, w_in, w_out, gain,
    full, out, wide, rows, send, land, hop, passed, near, c0, c1, g0, g1, s0, s1, s2, r0, r1,
):
    doms, size = mid.shape[0], mid.shape[1]
    net = Net(doms, groups)
    net.greet()
    net.meet()
    reduce = Reduce(net, part, hop, passed, near, (c0, c1), chunks)
    reduce.run()
    quarter = part.shape[1]
    full[net.e] = node_mlp(
        nodes[net.e], reduce.value(pl.ds(0, quarter)), w_in[1], w_out[1], gain[1:2, :]
    )
    wide[pl.ds(4 * quarter, 8), :] = jnp.zeros((8, LANES), F32)
    Relay(net, full, (g0, g1), 1).run()
    for q in range(4):
        wide[pl.ds(q * quarter, quarter), :] = full[q].astype(F32)
    exchange = Exchange(
        net, net.ahead,
        lambda t, peer: send.at[peer],
        lambda t: land.at[t * net.per + net.local],
        lambda t, l: land.at[t * net.per + l],
        (s0, s1, s2),
    )

    def start(t):
        gather_blocks(index, lambda k: k * size, wide, rows, send, (net.ahead(t), net.per))
        exchange.send(t)

    exchange.loop(start)
    exchange.own().start()
    each = groups // pieces

    def ready(s):
        def run(t, carry):
            exchange.receive(t)
            return carry

        lax.fori_loop(s * each, (s + 1) * each, run, 0)
        if s == 0:
            exchange.own().wait()
        span = each * net.per
        block = slice(s * span, (s + 1) * span)
        out[net.e, block] = (land[block].astype(F32) + mid[block].astype(F32)).astype(BF16)

    Relay(net, out, (r0, r1), pieces).run(ready)
    exchange.loop(lambda t: exchange.each(t, lambda i: exchange.copy(t, i).wait_send()))


def unpool_stage(groups, index, part, nodes, mid, w_in, w_out, gain, chunks=2, pieces=4):
    quarter, (doms, size, _) = part.shape[1], mid.shape
    pieces = min(pieces, groups)
    return pl.pallas_call(
        functools.partial(unpool_kernel, groups, chunks, pieces),
        out_shape=(
            jax.ShapeDtypeStruct(part.shape, BF16),
            jax.ShapeDtypeStruct((4,) + mid.shape, BF16),
        ),
        in_specs=[SMEM] + [VMEM] * 6,
        out_specs=(VMEM, VMEM),
        scratch_shapes=[
            pltpu.VMEM((4 * quarter + 8, LANES), F32),
            pltpu.VMEM((doms * size, LANES), F32),
            pltpu.VMEM(mid.shape, BF16),
            pltpu.VMEM(mid.shape, BF16),
        ]
        + reduce_scratch(quarter, chunks)
        + relay_sems(1)
        + exchange_sems(doms)
        + relay_sems(pieces),
        compiler_params=comm_params(3),
        name="unpool_stage",
    )(index, part, nodes, mid, w_in, w_out, gain)


def child_counts(dest, rows):
    high, low = dest // LANES, lax.rem(dest, LANES)
    left = (lax.broadcasted_iota(jnp.int32, (rows // LANES, dest.shape[0]), 0) == high[None, :]).astype(BF16)
    right = (lax.broadcasted_iota(jnp.int32, (LANES, dest.shape[0]), 0) == low[None, :]).astype(BF16)
    return lax.dot_general(left, right, (((1,), (1,)), ((), ())), preferred_element_type=F32)


def shards(groups, coarse_rows, *args):
    (
        fine_nodes, fine_edges, fine_senders, fine_receivers, fine_halo,
        coarse_edges, coarse_senders, coarse_receivers, coarse_halo,
        pool_send, pool_dest, unpool_slot,
        edge_in_weight, edge_out_weight, node_in_weight, node_out_weight, edge_gain, node_gain,
    ) = args
    e, me = lax.axis_index("edge"), lax.axis_index("dom")
    doms = fine_halo.shape[1]
    per = doms // groups

    def nearby(p):
        away = lax.rem(me // per + groups - p // per, groups)
        step = jnp.where(2 * away <= groups, jnp.maximum(2 * away - 1, 0), 2 * (groups - away))
        return step * per + lax.rem(p, per)

    def moved(senders, rows, width):
        far = senders - rows
        size = width // 4
        owner, slot = far // width, lax.rem(far, width)
        there = rows + (slot // size) * (doms * size) + nearby(owner) * size + lax.rem(slot, size)
        return jnp.where(senders < rows, senders, there)

    slots = pool_dest.shape[2]
    own_size = slots // 4
    slot = lax.rem(unpool_slot, slots)
    place = (slot // own_size) * (doms * own_size) + nearby(unpool_slot // slots) * own_size + lax.rem(slot, own_size)
    dest = lax.dynamic_slice_in_dim(pool_dest[0], e * own_size, own_size, axis=1).reshape(-1)
    senders = moved(fine_senders, fine_nodes.shape[0], fine_halo.shape[2])
    far_senders = moved(coarse_senders, coarse_rows, coarse_halo.shape[2])
    counts = child_counts(pool_dest[0].reshape(-1), coarse_rows).reshape(4, -1)
    counts = jnp.maximum(lax.dynamic_index_in_dim(counts, e, keepdims=False), 1.0)
    counts = jnp.broadcast_to(counts[:, None], (coarse_rows // 4, LANES))

    msg, own_nodes = message_stage(
        doms, groups, fine_halo.reshape(-1), pool_send.reshape(-1), senders, fine_receivers,
        fine_nodes, fine_edges, edge_in_weight, edge_out_weight, edge_gain,
    )
    part = sum_stage(fine_receivers, place, msg, doms * slots)
    mid, arrived = fine_stage(
        groups, part.reshape(4, -1, LANES), own_nodes, node_in_weight, node_out_weight, node_gain
    )
    pooled = pool_stage(dest, arrived.reshape(-1, LANES), coarse_rows)
    coarse_in, coarse_ghosts = coarse_border_stage(
        doms, groups, coarse_halo.reshape(-1), pooled.reshape(4, -1, LANES), counts
    )
    part = coarse_edge_stage(
        far_senders, coarse_receivers, coarse_in.reshape(-1, LANES), coarse_ghosts.reshape(-1, LANES),
        coarse_edges, edge_in_weight, edge_out_weight, edge_gain,
    )
    coarse_out, table = unpool_stage(
        groups, dest, part.reshape(4, -1, LANES), coarse_in, mid, node_in_weight, node_out_weight, node_gain
    )
    fine_out = final_stage(place, table.reshape(-1, LANES))
    return fine_out, coarse_out.reshape(-1, LANES)


def solution(mesh, groups=8, coarse_rows=2048):
    placed = (
        P("dom", None),
        P(("dom", "edge"), None),
        P(("dom", "edge")),
        P(("dom", "edge")),
        P("dom", None, None),
        P(("dom", "edge"), None),
        P(("dom", "edge")),
        P(("dom", "edge")),
        P("dom", None, None),
        P("dom", None, None),
        P("dom", None, None),
        P("dom"),
        P(),
        P(),
        P(),
        P(),
        P(),
        P(),
    )
    return jax.shard_map(
        functools.partial(shards, groups, coarse_rows),
        mesh=mesh,
        in_specs=placed,
        out_specs=(P("dom", None), P("dom", None)),
        check_vma=False,
    )
```

profile of v0, /device:TPU:1, one launch (start us, length us, event | category | flops | bytes accessed | tf_op | source)
XLA Modules:
  0.0 264.8 jit_solution(1763875329950425148)
XLA Ops:
  0.6 0.0 copy-start.2
  0.7 1.4 compare_select_fusion.senders
  2.0 1.5 reshape.90.pool_send
  3.6 1.4 reshape.89.halo
  5.0 47.8 %message_stage.1 = (f32[4096,128]{1,0:T(8,128)}, bf16[64,48,128]{2,1,0:T(8,128)(2,1)}) custom-call(s32[4096]{0:T(1024)} %reshape.89.halo, s32[12288]{0:T(1024)} %reshape.90.pool_send, s32[4096]{0:T(1024)} %compare_select_fusion.senders, s32[4096]{0:T(1024)} %receivers.4, bf16[8192,128]{1,0:T(8,128)(2,1)} %nodes.1, bf16[4096,128]{1,0:T(8,128)(2,1)} %edges.2, ...), custom_call_target="tpu_custom_call" | custom-call | tf_op jit(solution)/shard_map/message_stage/pallas_call | solution.py:536
  52.8 0.0 copy-done.2
  52.8 0.7 fusion.6.place.index
  53.5 13.5 %sum_stage.1 = bf16[12288,128]{1,0:T(8,128)(2,1)} custom-call(s32[4096]{0:T(1024)} %receivers.4, s32[8192]{0:T(1024)} %fusion.6.place.index, f32[4096,128]{1,0:T(8,128)} %get-tuple-element.10.msg), custom_call_target="tpu_custom_call" | custom-call | tf_op jit(solution)/shard_map/sum_stage/pallas_call | solution.py:151
  67.0 0.0 copy-start.1
  67.0 55.3 %fine_stage.1 = (bf16[64,48,128]{2,1,0:T(8,128)(2,1)}, bf16[64,48,128]{2,1,0:T(8,128)(2,1)}) custom-call(bf16[4,3072,128]{2,1,0:T(8,128)(2,1)} %bitcast.9, bf16[64,48,128]{2,1,0:T(8,128)(2,1)} %get-tuple-element.11.nodes, bf16[2,256,128]{2,1,0:T(8,128)(2,1)} %w_in.7, bf16[2,128,128]{2,1,0:T(8,128)(2,1)} %w_out.7, f32[2,128]{1,0:T(2,128)} %gain.7), custom_call_target="tpu_custom_call" | custom-call | tf_op jit(solution)/shard_map/fine_stage/pallas_call | solution.py:592
  122.4 0.0 copy-start.3
  122.4 0.0 copy-done.1
  122.4 0.1 constant_dynamic-slice_fusion
  122.5 0.7 reshape.87.dest.index
  123.1 0.0 copy-start.4
  123.1 8.1 %pool_stage.1 = bf16[2048,128]{1,0:T(8,128)(2,1)} custom-call(s32[3072]{0:T(1024)} %reshape.87.dest.index, bf16[3072,128]{1,0:T(8,128)(2,1)} %bitcast.14), custom_call_target="tpu_custom_call" | custom-call | tf_op jit(solution)/shard_map/pool_stage/pallas_call | solution.py:169
  131.3 0.1 reshape_squeeze.3
  131.4 1.1 fusion
  132.6 0.8 broadcast_in_dim.2.count
  133.4 0.0 copy-done.3
  133.4 0.1 copy.20
  133.5 0.7 reshape.88.halo
  134.2 41.4 %coarse_border_stage.1 = (bf16[4,512,128]{2,1,0:T(8,128)(2,1)}, bf16[4,64,8,128]{3,2,1,0:T(8,128)(2,1)}) custom-call(s32[2048]{0:T(1024)} %reshape.88.halo, bf16[4,512,128]{2,1,0:T(8,128)(2,1)} %bitcast.11, f32[512,128]{1,0:T(8,128)} %broadcast_in_dim.2.count), custom_call_target="tpu_custom_call" | custom-call | tf_op jit(solution)/shard_map/coarse_border_stage/pallas_call | solution.py:635
  175.6 0.0 copy-done.4
  175.6 0.6 compare_select_fusion.1.senders
  176.2 9.0 %coarse_edge_stage.1 = bf16[2048,128]{1,0:T(8,128)(2,1)} custom-call(s32[1024]{0:T(1024)} %compare_select_fusion.1.senders, s32[1024]{0:T(1024)} %receivers.5, bf16[2048,128]{1,0:T(8,128)(2,1)} %bitcast.12, bf16[2048,128]{1,0:T(8,128)(2,1)} %bitcast.16, bf16[1024,128]{1,0:T(8,128)(2,1)} %edges.3, bf16[2,384,128]{2,1,0:T(8,128)(2,1)} %w_in.6, ...), custom_call_target="tpu_custom_call" | custom-call | tf_op jit(solution)/shard_map/coarse_edge_stage/pallas_call | solution.py:129
  185.2 67.6 %unpool_stage.1 = (bf16[4,512,128]{2,1,0:T(8,128)(2,1)}, bf16[4,64,48,128]{3,2,1,0:T(8,128)(2,1)}) custom-call(s32[3072]{0:T(1024)} %reshape.87.dest.index, bf16[4,512,128]{2,1,0:T(8,128)(2,1)} %bitcast.13, bf16[4,512,128]{2,1,0:T(8,128)(2,1)} %get-tuple-element.13.nodes, bf16[64,48,128]{2,1,0:T(8,128)(2,1)} %get-tuple-element.15.mid, ...), custom_call_target="tpu_custom_call" | custom-call | tf_op jit(solution)/shard_map/unpool_stage/pallas_call | solution.py:710
  252.9 0.0 copy-start
  252.9 11.1 %final_stage.1 = bf16[8192,128]{1,0:T(8,128)(2,1)} custom-call(s32[8192]{0:T(1024)} %fusion.6.place.index, bf16[12288,128]{1,0:T(8,128)(2,1)} %bitcast.10), custom_call_target="tpu_custom_call" | custom-call | tf_op jit(solution)/shard_map/final_stage/pallas_call | solution.py:191
  264.0 0.0 copy-done
  264.0 0.8 copy.22
  (3 shorter events, 0.1 us)
Async XLA Ops:
  0.6 52.2 %copy-start.2 = (s32[8192]{0:T(1024)S(1)}, s32[8192]{0:T(1024)}, u32[]{:S(2)}) copy-start(s32[8192]{0:T(1024)} %param.29) | copy-start | bytes 98308
  67.0 55.4 %copy-start.1 = (s32[1,64,192]{2,1,0:T(8,128)S(1)}, s32[1,64,192]{2,1,0:T(8,128)}, u32[]{:S(2)}) copy-start(s32[1,64,192]{2,1,0:T(8,128)} %param.28) | copy-start | bytes 147460
  122.4 11.1 %copy-start.3 = (s32[1,64,32]{1,2,0:T(8,128)S(1)}, s32[1,64,32]{1,2,0:T(8,128)}, u32[]{:S(2)}) copy-start(s32[1,64,32]{1,2,0:T(8,128)} %param.26) | copy-start | bytes 24580
  123.1 52.5 %copy-start.4 = (s32[1024]{0:T(1024)S(1)}, s32[1024]{0:T(1024)}, u32[]{:S(2)}) copy-start(s32[1024]{0:T(1024)} %param.24) | copy-start | bytes 12292
  252.9 11.1 %copy-start = (bf16[4,512,128]{2,1,0:T(8,128)(2,1)S(1)}, bf16[4,512,128]{2,1,0:T(8,128)(2,1)}, u32[]{:S(2)}) copy-start(bf16[4,512,128]{2,1,0:T(8,128)(2,1)} %get-tuple-element.17) | copy-start | bytes 1572868
where the time goes:
time: 265 us
  Pallas kernels  254 us (96%)
  local copies, waits for them, and re-layouts  6.26 us (2%)
  other arithmetic  2.74 us (1%)
    pallas_call x1, Pallas kernels, unpool_stage(): pl.pallas_call(functools.partial(unpool_kernel, groups, chunks, pieces),...  67.6 us
    pallas_call x1, Pallas kernels, fine_stage(): pl.pallas_call(functools.partial(fine_kernel, groups), out_shape=(jax.Sha...  55.3 us
    pallas_call x1, Pallas kernels, message_stage(): pl.pallas_call(functools.partial(message_kernel, groups, pieces), out_sha...  47.8 us
    pallas_call x1, Pallas kernels, coarse_border_stage(): pl.pallas_call(functools.partial(coarse_border_kernel, groups, chunks), o...  41.4 us
    pallas_call x1, Pallas kernels, sum_stage(): pl.pallas_call(sum_kernel, out_shape=jax.ShapeDtypeStruct((slots, LANES),...  13.5 us
    pallas_call x1, Pallas kernels, final_stage(): pl.pallas_call(final_kernel, out_shape=jax.ShapeDtypeStruct((count, LANES...  11.1 us
    pallas_call x1, Pallas kernels, coarse_edge_stage(): pl.pallas_call(coarse_edge_kernel, out_shape=jax.ShapeDtypeStruct((rows,...  8.99 us
    pallas_call x1, Pallas kernels, pool_stage(): pl.pallas_call(pool_kernel, out_shape=jax.ShapeDtypeStruct((rows, LANES),...  8.14 us

commit v1 on v0

--- a/solution.py
+++ b/solution.py
@@ -64,16 +64,11 @@
     row_loop(accs[0].shape[0] // step * step, step, body)
 
 
-def add_rows(where, values, count, accs, unroll=16):
+def add_rows(where, values, count, accs, unroll=32):
     def body(at):
-        for j in range(0, unroll, 2):
-            acc = accs[(j // 2) % len(accs)]
-            first, second = where(at + j), where(at + j + 1)
-            value = acc[pl.ds(first, 1), :] + values[pl.ds(at + j, 1), :]
-            other = acc[pl.ds(second, 1), :]
-            other = jnp.where(first == second, value, other) + values[pl.ds(at + j + 1, 1), :]
-            acc[pl.ds(first, 1), :] = value
-            acc[pl.ds(second, 1), :] = other
+        for j in range(unroll):
+            acc, row = accs[j % len(accs)], where(at + j)
+            acc[pl.ds(row, 1), :] = acc[pl.ds(row, 1), :] + values[pl.ds(at + j, 1), :]
 
     row_loop(count, unroll, body)
 
@@ -103,44 +98,6 @@
     row_loop(msg.shape[0], step, body)
 
 
-def coarse_edge_kernel(senders, receivers, nodes, ghosts, edges, w_in, w_out, gain, out, table_s, table_r, msg, *accs):
-    rows, count = nodes.shape[0], edges.shape[0]
-    w = w_in[1]
-    premultiply(nodes, w[0:LANES, :], table_s)
-    premultiply(nodes, w[LANES : 2 * LANES, :], table_r)
-    premultiply(ghosts, w[0:LANES, :], table_s, rows)
-    premultiply(edges, w[2 * LANES :, :], msg)
-    clear_all(accs)
-
-    def gather(at):
-        for j in range(32):
-            msg[pl.ds(at + j, 1), :] = msg[pl.ds(at + j, 1), :] + (
-                table_s[pl.ds(senders[at + j], 1), :] + table_r[pl.ds(receivers[at + j], 1), :]
-            )
-
-    row_loop(count, 32, gather)
-    edge_mlp(msg, w_out[1], gain[1:2, :], msg)
-    add_rows(lambda j: receivers[j], msg, count, accs)
-    sum_accs(accs, out)
-
-
-def coarse_edge_stage(senders, receivers, nodes, ghosts, edges, w_in, w_out, gain):
-    rows, far, count = nodes.shape[0], ghosts.shape[0], edges.shape[0]
-    return pl.pallas_call(
-        coarse_edge_kernel,
-        out_shape=jax.ShapeDtypeStruct((rows, LANES), BF16),
-        in_specs=[SMEM] * 2 + [VMEM] * 6,
-        out_specs=VMEM,
-        scratch_shapes=[
-            pltpu.VMEM((rows + far, LANES), F32),
-            pltpu.VMEM((rows, LANES), F32),
-            pltpu.VMEM((count, LANES), F32),
-        ]
-        + [pltpu.VMEM((rows, LANES), F32)] * 2,
-        name="coarse_edge_stage",
-    )(senders, receivers, nodes, ghosts, edges, w_in, w_out, gain)
-
-
 def sum_kernel(receivers, place, msg, out, *accs):
     clear_all(accs)
     add_rows(lambda j: place[receivers[j]], msg, msg.shape[0], accs)
@@ -153,27 +110,9 @@
         out_shape=jax.ShapeDtypeStruct((slots, LANES), BF16),
         in_specs=[SMEM, SMEM, VMEM],
         out_specs=VMEM,
-        scratch_shapes=[pltpu.VMEM((slots, LANES), F32)] * 2,
+        scratch_shapes=[pltpu.VMEM((slots, LANES), F32)] * 3,
         name="sum_stage",
     )(receivers, place, msg)
-
-
-def pool_kernel(dest, arrived, out, wide, *accs):
-    clear_all(accs)
-    widen(arrived, wide)
-    add_rows(lambda j: dest[j], wide, arrived.shape[0], accs)
-    sum_accs(accs, out)
-
-
-def pool_stage(dest, arrived, rows):
-    return pl.pallas_call(
-        pool_kernel,
-        out_shape=jax.ShapeDtypeStruct((rows, LANES), BF16),
-        in_specs=[SMEM, VMEM],
-        out_specs=VMEM,
-        scratch_shapes=[pltpu.VMEM(arrived.shape, F32)] + [pltpu.VMEM((rows + 8, LANES), F32)] * 2,
-        name="pool_stage",
-    )(dest, arrived)
 
 
 def final_kernel(index, table, out, wide, rows):
@@ -418,17 +357,20 @@
         for copy in (self.raw_right(c), self.raw_left(c), self.sum_right(c), self.sum_left(c)):
             copy.wait()
 
-    def run(self, use=lambda c: None):
-        self.start(0)
-        for c in range(self.chunks):
-            if c + 1 < self.chunks:
-                self.start(c + 1)
+    def run(self, use=lambda c: None, aside=lambda: None):
+        order = list(reversed(range(self.chunks)))
+        self.start(order[0])
+        for k, c in enumerate(order):
+            if k + 1 < self.chunks:
+                self.start(order[k + 1])
+            if k == 0:
+                aside()
             self.through(c)
-            if c:
-                self.finish(c - 1)
-                use(c - 1)
-        self.finish(self.chunks - 1)
-        use(self.chunks - 1)
+            if k:
+                self.finish(order[k - 1])
+                use(order[k - 1])
+        self.finish(order[-1])
+        use(order[-1])
 
     def value(self, rows):
         return (
@@ -557,184 +499,231 @@
     )(halo, pool_send, senders, receivers, nodes, edges, w_in, w_out, gain)
 
 
-def fine_kernel(groups, part, nodes, w_in, w_out, gain, mid, arrived, hop, passed, near, c0, c1, s0, s1, s2):
+def child_counts(all_dest, first, counts, step=128):
+    lines = all_dest.shape[0]
+
+    def rows(at):
+        target = lax.broadcasted_iota(jnp.int32, (step, LANES), 0) + (first + at)
+
+        def line(i, total):
+            for j in range(8):
+                hit = all_dest[pl.ds(i * 8 + j, 1), :] == target
+                total = total + jnp.where(hit, 1.0, 0.0)
+            return total
+
+        total = lax.fori_loop(0, lines // 8, line, jnp.zeros((step, LANES), F32))
+        counts[pl.ds(at, step), :] = jnp.broadcast_to(jnp.sum(total, axis=1, keepdims=True), (step, LANES))
+
+    row_loop(counts.shape[0], step, rows)
+
+
+def one_hot(index, first, rows):
+    at = lax.broadcasted_iota(jnp.int32, (rows, index.shape[1]), 0) + first
+    return jnp.where(at == index, 1.0, 0.0).astype(BF16)
+
+
+def main_kernel(
+    groups, pieces, halo, dest, senders, receivers, all_dest, group_dest, line_receivers,
+    part, nodes, edges, edge_in, edge_out, node_in, node_out, edge_gain, node_gain,
+    coarse_out, table,
+    hop, passed, near, mid, arrived, counts, pooled, coarse_part, coarse_hop, coarse_passed, coarse_near,
+    coarse_in, ghosts, wide, rows, border, table_s, table_r, msg, send, land,
+    f0, f1, p0, p1, e0, e1, a0, a1, b0, b1, g0, g1, h0, h1, i0, i1, i2, j0, j1, j2, k0, k1, k2,
+):
     doms, size = mid.shape[0], mid.shape[1]
+    quarter, border_size = coarse_in.shape[1], ghosts.shape[2]
+    coarse_rows, count = 4 * quarter, edges.shape[0]
     net = Net(doms, groups)
     net.greet()
+    premultiply(edges, edge_in[1, 2 * LANES :, :], msg)
     net.meet()
-    reduce = Reduce(net, part, hop, passed, near, (c0, c1), groups // 2)
-    exchange = Exchange(
+
+    reduce = Reduce(net, part, hop, passed, near, (f0, f1), groups // 2)
+    pool = Exchange(
         net, net.behind,
         lambda t, peer: mid.at[t * net.per + lax.rem(peer, net.per)],
         lambda t: arrived.at[net.me],
         lambda t, l: arrived.at[net.ahead(t) + l],
-        (s0, s1, s2),
+        (i0, i1, i2),
     )
     span = net.per * size
 
     def use(c):
-        units = (c, groups // 2 + c)
+        units = (groups // 2 + c, c)
         for u in units:
             own = nodes[u * net.per : (u + 1) * net.per].reshape(span, LANES)
-            result = node_mlp(own, reduce.value(pl.ds(u * span, span)), w_in[0], w_out[0], gain[0:1, :])
+            result = node_mlp(own, reduce.value(pl.ds(u * span, span)), node_in[0], node_out[0], node_gain[0:1, :])
             mid[u * net.per : (u + 1) * net.per] = result.reshape(net.per, size, LANES)
         if c == 0:
-            exchange.own().start()
+            pool.own().start()
         for u in units:
-            exchange.send(u)
-
-    reduce.run(use)
+            pool.send(u)
+
+    def aside():
+        pooled[...] = jnp.zeros_like(pooled)
+        child_counts(all_dest, net.e * quarter, counts)
+
+    reduce.run(use, aside)
+
+    def gathered(k, carry):
+        c = groups // 2 - 1 - k // 2
+        t = c + (1 - lax.rem(k, 2)) * (groups // 2)
+        pool.receive(t)
+
+        @pl.when(t == 0)
+        def _():
+            pool.own().wait()
+
+        first = net.ahead(t)
+        block = arrived[pl.ds(first, net.per)].reshape(span, LANES)
+        index = group_dest[pl.ds(first // net.per, 1), :]
+        for q in range(4):
+            at = pl.ds(q * quarter, quarter)
+            pooled[at, :] = pooled[at, :] + dot(one_hot(index, q * quarter, quarter), block)
+        return carry
+
+    lax.fori_loop(0, groups, gathered, 0)
+    for owner in (net.opp, net.right, net.left, net.e):
+        at = pl.ds(pl.multiple_of(owner * quarter, quarter), quarter)
+        coarse_part[owner] = pooled[at, :].astype(BF16)
+    pool.loop(lambda t: pool.each(t, lambda i: pool.copy(t, i).wait_send()))
+
+    reduce = Reduce(net, coarse_part, coarse_hop, coarse_passed, coarse_near, (p0, p1), p0.shape[1])
+    reduce.run()
+    mean = reduce.value(pl.ds(0, quarter)) / jnp.maximum(counts[...], 1.0)
+    coarse_in[net.e] = mean.astype(BF16)
+    Relay(net, coarse_in, (g0, g1), 1).run()
+    for q in range(4):
+        wide[pl.ds(q * quarter, quarter), :] = coarse_in[q].astype(F32)
+    gather_blocks(halo, lambda k: k * (4 * border_size) + net.e * border_size, wide, rows, border, (0, doms))
+    here = ghosts.at[net.e]
+    exchange = Exchange(
+        net, net.ahead,
+        lambda t, peer: border.at[peer],
+        lambda t: here.at[t * net.per + net.local],
+        lambda t, l: here.at[t * net.per + l],
+        (j0, j1, j2),
+    )
+    exchange.own().start()
+    exchange.loop(exchange.send)
+    w = edge_in[1]
+    for q in range(4):
+        table_r[pl.ds(q * quarter, quarter), :] = dot(coarse_in[q], w[LANES : 2 * LANES, :])
+        table_s[pl.ds(q * quarter, quarter), :] = dot(coarse_in[q], w[0:LANES, :])
+
+    def gather_near(at):
+        for j in range(32):
+            msg[pl.ds(at + j, 1), :] = msg[pl.ds(at + j, 1), :] + table_r[pl.ds(receivers[at + j], 1), :]
+
+    row_loop(count, 32, gather_near)
     exchange.loop(exchange.receive)
     exchange.finish()
-
-
-def fine_stage(groups, part, nodes, w_in, w_out, gain):
-    return pl.pallas_call(
-        functools.partial(fine_kernel, groups),
-        out_shape=(jax.ShapeDtypeStruct(nodes.shape, BF16), jax.ShapeDtypeStruct(nodes.shape, BF16)),
-        in_specs=[VMEM] * 5,
-        out_specs=(VMEM, VMEM),
-        scratch_shapes=reduce_scratch(part.shape[1], groups // 2) + exchange_sems(nodes.shape[0]),
-        compiler_params=comm_params(1),
-        name="fine_stage",
-    )(part, nodes, w_in, w_out, gain)
-
-
-def coarse_border_kernel(
-    groups, chunks, halo, part, count, full, out, wide, rows, send, hop, passed, near, c0, c1, g0, g1, s0, s1, s2, r0, r1
-):
-    doms, size = out.shape[1], out.shape[2]
-    net = Net(doms, groups)
-    net.greet()
-    net.meet()
-    reduce = Reduce(net, part, hop, passed, near, (c0, c1), chunks)
+    Relay(net, ghosts, (h0, h1), 1).run()
+    for owner in range(4):
+        block = ghosts[owner].reshape(doms * border_size, LANES)
+        at = pl.ds(coarse_rows + owner * doms * border_size, doms * border_size)
+        table_s[at, :] = dot(block, w[0:LANES, :])
+
+    def gather_far(at):
+        for j in range(32):
+            msg[pl.ds(at + j, 1), :] = msg[pl.ds(at + j, 1), :] + table_s[pl.ds(senders[at + j], 1), :]
+
+    row_loop(count, 32, gather_far)
+    edge_mlp(msg, edge_out[1], edge_gain[1:2, :], msg)
+    high = msg[...].astype(BF16)
+    low = (msg[...] - high.astype(F32)).astype(BF16)
+    both = jnp.concatenate([high, low], axis=1)
+    for owner in (net.opp, net.right, net.left, net.e):
+        sums = dot(one_hot(line_receivers[...], owner * quarter, quarter), both)
+        coarse_part[owner] = (sums[:, 0:LANES] + sums[:, LANES:]).astype(BF16)
+
+    reduce = Reduce(net, coarse_part, coarse_hop, coarse_passed, coarse_near, (e0, e1), e0.shape[1])
     reduce.run()
-    quarter = part.shape[1]
-    full[net.e] = (reduce.value(pl.ds(0, quarter)) / count[...]).astype(BF16)
-    Relay(net, full, (g0, g1), 1).run()
+    coarse_out[net.e] = node_mlp(
+        coarse_in[net.e], reduce.value(pl.ds(0, quarter)), node_in[1], node_out[1], node_gain[1:2, :]
+    )
+    wide[pl.ds(coarse_rows, 8), :] = jnp.zeros((8, LANES), F32)
+    Relay(net, coarse_out, (a0, a1), 1).run()
     for q in range(4):
-        wide[pl.ds(q * quarter, quarter), :] = full[q].astype(F32)
-    gather_blocks(halo, lambda k: k * (4 * size) + net.e * size, wide, rows, send, (0, doms))
-    land = out.at[net.e]
-    exchange = Exchange(
+        wide[pl.ds(q * quarter, quarter), :] = coarse_out[q].astype(F32)
+    back = Exchange(
         net, net.ahead,
         lambda t, peer: send.at[peer],
         lambda t: land.at[t * net.per + net.local],
         lambda t, l: land.at[t * net.per + l],
-        (s0, s1, s2),
-    )
-    exchange.own().start()
-    exchange.loop(exchange.send)
-    exchange.loop(exchange.receive)
-    exchange.finish()
-    Relay(net, out, (r0, r1), 1).run()
-
-
-def coarse_border_stage(doms, groups, halo, part, count, chunks=2):
-    quarter, size = part.shape[1], halo.shape[0] // doms // 4
+        (k0, k1, k2),
+    )
+
+    def start(t):
+        gather_blocks(dest, lambda k: k * size, wide, rows, send, (net.ahead(t), net.per))
+        back.send(t)
+
+    back.loop(start)
+    back.own().start()
+    each = groups // pieces
+
+    def ready(s):
+        def run(t, carry):
+            back.receive(t)
+            return carry
+
+        lax.fori_loop(s * each, (s + 1) * each, run, 0)
+        if s == 0:
+            back.own().wait()
+        block = slice(s * each * net.per, (s + 1) * each * net.per)
+        table[net.e, block] = (land[block].astype(F32) + mid[block].astype(F32)).astype(BF16)
+
+    Relay(net, table, (b0, b1), pieces).run(ready)
+    back.loop(lambda t: back.each(t, lambda i: back.copy(t, i).wait_send()))
+
+
+def main_stage(groups, coarse_rows, ints, part, nodes, edges, weights, pieces=4):
+    doms, size, _ = nodes.shape
+    pieces, quarter = min(pieces, groups), coarse_rows // 4
+    border_size, count = ints[0].shape[0] // doms // 4, edges.shape[0]
+    vmem = pltpu.VMEM
     return pl.pallas_call(
-        functools.partial(coarse_border_kernel, groups, chunks),
+        functools.partial(main_kernel, groups, pieces),
         out_shape=(
-            jax.ShapeDtypeStruct(part.shape, BF16),
-            jax.ShapeDtypeStruct((4, doms, size, LANES), BF16),
+            jax.ShapeDtypeStruct((4, quarter, LANES), BF16),
+            jax.ShapeDtypeStruct((4,) + nodes.shape, BF16),
         ),
-        in_specs=[SMEM, VMEM, VMEM],
+        in_specs=[SMEM] * 4 + [VMEM] * 12,
         out_specs=(VMEM, VMEM),
-        scratch_shapes=[
-            pltpu.VMEM((4 * quarter, LANES), F32),
-            pltpu.VMEM((doms * size, LANES), F32),
-            pltpu.VMEM((doms, size, LANES), BF16),
+        scratch_shapes=reduce_scratch(part.shape[1], 1)[:3]
+        + [
+            vmem(nodes.shape, BF16),
+            vmem(nodes.shape, BF16),
+            vmem((quarter, LANES), F32),
+            vmem((coarse_rows, LANES), F32),
+            vmem((4, quarter, LANES), BF16),
         ]
-        + reduce_scratch(quarter, chunks)
+        + reduce_scratch(quarter, 1)[:3]
+        + [
+            vmem((4, quarter, LANES), BF16),
+            vmem((4, doms, border_size, LANES), BF16),
+            vmem((coarse_rows + 8, LANES), F32),
+            vmem((doms * size, LANES), F32),
+            vmem((doms, border_size, LANES), BF16),
+            vmem((coarse_rows + 4 * doms * border_size, LANES), F32),
+            vmem((coarse_rows, LANES), F32),
+            vmem((count, LANES), F32),
+            vmem(nodes.shape, BF16),
+            vmem(nodes.shape, BF16),
+        ]
+        + reduce_scratch(quarter, groups // 2)[3:]
+        + reduce_scratch(quarter, 2)[3:]
+        + reduce_scratch(quarter, 2)[3:]
+        + relay_sems(1)
+        + relay_sems(pieces)
+        + relay_sems(1)
         + relay_sems(1)
         + exchange_sems(doms)
-        + relay_sems(1),
-        compiler_params=comm_params(2),
-        name="coarse_border_stage",
-    )(halo, part, count)
-
-
-def unpool_kernel(
-    groups, chunks, pieces, index, part, nodes, mid, w_in, w_out, gain,
-    full, out, wide, rows, send, land, hop, passed, near, c0, c1, g0, g1, s0, s1, s2, r0, r1,
-):
-    doms, size = mid.shape[0], mid.shape[1]
-    net = Net(doms, groups)
-    net.greet()
-    net.meet()
-    reduce = Reduce(net, part, hop, passed, near, (c0, c1), chunks)
-    reduce.run()
-    quarter = part.shape[1]
-    full[net.e] = node_mlp(
-        nodes[net.e], reduce.value(pl.ds(0, quarter)), w_in[1], w_out[1], gain[1:2, :]
-    )
-    wide[pl.ds(4 * quarter, 8), :] = jnp.zeros((8, LANES), F32)
-    Relay(net, full, (g0, g1), 1).run()
-    for q in range(4):
-        wide[pl.ds(q * quarter, quarter), :] = full[q].astype(F32)
-    exchange = Exchange(
-        net, net.ahead,
-        lambda t, peer: send.at[peer],
-        lambda t: land.at[t * net.per + net.local],
-        lambda t, l: land.at[t * net.per + l],
-        (s0, s1, s2),
-    )
-
-    def start(t):
-        gather_blocks(index, lambda k: k * size, wide, rows, send, (net.ahead(t), net.per))
-        exchange.send(t)
-
-    exchange.loop(start)
-    exchange.own().start()
-    each = groups // pieces
-
-    def ready(s):
-        def run(t, carry):
-            exchange.receive(t)
-            return carry
-
-        lax.fori_loop(s * each, (s + 1) * each, run, 0)
-        if s == 0:
-            exchange.own().wait()
-        span = each * net.per
-        block = slice(s * span, (s + 1) * span)
-        out[net.e, block] = (land[block].astype(F32) + mid[block].astype(F32)).astype(BF16)
-
-    Relay(net, out, (r0, r1), pieces).run(ready)
-    exchange.loop(lambda t: exchange.each(t, lambda i: exchange.copy(t, i).wait_send()))
-
-
-def unpool_stage(groups, index, part, nodes, mid, w_in, w_out, gain, chunks=2, pieces=4):
-    quarter, (doms, size, _) = part.shape[1], mid.shape
-    pieces = min(pieces, groups)
-    return pl.pallas_call(
-        functools.partial(unpool_kernel, groups, chunks, pieces),
-        out_shape=(
-            jax.ShapeDtypeStruct(part.shape, BF16),
-            jax.ShapeDtypeStruct((4,) + mid.shape, BF16),
-        ),
-        in_specs=[SMEM] + [VMEM] * 6,
-        out_specs=(VMEM, VMEM),
-        scratch_shapes=[
-            pltpu.VMEM((4 * quarter + 8, LANES), F32),
-            pltpu.VMEM((doms * size, LANES), F32),
-            pltpu.VMEM(mid.shape, BF16),
-            pltpu.VMEM(mid.shape, BF16),
-        ]
-        + reduce_scratch(quarter, chunks)
-        + relay_sems(1)
         + exchange_sems(doms)
-        + relay_sems(pieces),
-        compiler_params=comm_params(3),
-        name="unpool_stage",
-    )(index, part, nodes, mid, w_in, w_out, gain)
-
-
-def child_counts(dest, rows):
-    high, low = dest // LANES, lax.rem(dest, LANES)
-    left = (lax.broadcasted_iota(jnp.int32, (rows // LANES, dest.shape[0]), 0) == high[None, :]).astype(BF16)
-    right = (lax.broadcasted_iota(jnp.int32, (LANES, dest.shape[0]), 0) == low[None, :]).astype(BF16)
-    return lax.dot_general(left, right, (((1,), (1,)), ((), ())), preferred_element_type=F32)
+        + exchange_sems(doms),
+        compiler_params=comm_params(1),
+        name="main_stage",
+    )(*ints, part, nodes, edges, *weights)
 
 
 def shards(groups, coarse_rows, *args):
@@ -767,28 +756,19 @@
     dest = lax.dynamic_slice_in_dim(pool_dest[0], e * own_size, own_size, axis=1).reshape(-1)
     senders = moved(fine_senders, fine_nodes.shape[0], fine_halo.shape[2])
     far_senders = moved(coarse_senders, coarse_rows, coarse_halo.shape[2])
-    counts = child_counts(pool_dest[0].reshape(-1), coarse_rows).reshape(4, -1)
-    counts = jnp.maximum(lax.dynamic_index_in_dim(counts, e, keepdims=False), 1.0)
-    counts = jnp.broadcast_to(counts[:, None], (coarse_rows // 4, LANES))
 
     msg, own_nodes = message_stage(
         doms, groups, fine_halo.reshape(-1), pool_send.reshape(-1), senders, fine_receivers,
         fine_nodes, fine_edges, edge_in_weight, edge_out_weight, edge_gain,
     )
     part = sum_stage(fine_receivers, place, msg, doms * slots)
-    mid, arrived = fine_stage(
-        groups, part.reshape(4, -1, LANES), own_nodes, node_in_weight, node_out_weight, node_gain
-    )
-    pooled = pool_stage(dest, arrived.reshape(-1, LANES), coarse_rows)
-    coarse_in, coarse_ghosts = coarse_border_stage(
-        doms, groups, coarse_halo.reshape(-1), pooled.reshape(4, -1, LANES), counts
-    )
-    part = coarse_edge_stage(
-        far_senders, coarse_receivers, coarse_in.reshape(-1, LANES), coarse_ghosts.reshape(-1, LANES),
-        coarse_edges, edge_in_weight, edge_out_weight, edge_gain,
-    )
-    coarse_out, table = unpool_stage(
-        groups, dest, part.reshape(4, -1, LANES), coarse_in, mid, node_in_weight, node_out_weight, node_gain
+    ints = (
+        coarse_halo.reshape(-1), dest, far_senders, coarse_receivers,
+        pool_dest.reshape(-1, LANES), dest.reshape(groups, -1), coarse_receivers.reshape(1, -1),
+    )
+    weights = (edge_in_weight, edge_out_weight, node_in_weight, node_out_weight, edge_gain, node_gain)
+    coarse_out, table = main_stage(
+        groups, coarse_rows, ints, part.reshape(4, -1, LANES), own_nodes, coarse_edges, weights
     )
     fine_out = final_stage(place, table.reshape(-1, LANES))
     return fine_out, coarse_out.reshape(-1, LANES)

time: 265 us -> 236 us (0.89)
  Pallas kernels: 254 us -> 220 us
  local copies, waits for them, and re-layouts: 6.26 us -> 9.05 us
    pallas_call x5 -> x1, Pallas kernels: 182 us -> 149 us  [main_stage(): pl.pallas_call(functools.partial(main_kernel, groups, pieces), out_shape=...]
where the time goes in v1:
time: 236 us; the launch traced here: 234 us
  Pallas kernels  220 us (93%)
  local copies, waits for them, and re-layouts  9.05 us (4%)
  other arithmetic  4.14 us (2%)
    pallas_call x1, Pallas kernels, main_stage(): pl.pallas_call(functools.partial(main_kernel, groups, pieces), out_shape=...  149 us
    pallas_call x1, Pallas kernels, message_stage(): pl.pallas_call(functools.partial(message_kernel, groups, pieces), out_sha...  47.8 us
    pallas_call x1, Pallas kernels, sum_stage(): pl.pallas_call(sum_kernel, out_shape=jax.ShapeDtypeStruct((slots, LANES),...  12.8 us
    pallas_call x1, Pallas kernels, final_stage(): pl.pallas_call(final_kernel, out_shape=jax.ShapeDtypeStruct((count, LANES...  11.1 us

profile of v1, /device:TPU:1, one launch (start us, length us, event | category | flops | bytes accessed | tf_op | source)
XLA Modules:
  0.0 234.1 jit_solution(2112477633016598545)
XLA Ops:
  0.6 1.3 compare_select_fusion.1.senders
  2.0 1.4 compare_select_fusion.senders
  3.3 1.4 reshape.38.halo
  4.8 1.5 fusion.2.place.index
  6.2 0.9 constant_dynamic-slice_fusion
  7.1 0.7 reshape_reshape.3.group_dest
  7.8 0.7 reshape.35.dest
  8.5 0.8 copy.20
  9.3 0.7 reshape.34.halo
  9.9 1.5 reshape.39.pool_send
  11.5 1.5 reshape.36.all_dest
  13.0 47.8 %message_stage.1 = (f32[4096,128]{1,0:T(8,128)}, bf16[64,48,128]{2,1,0:T(8,128)(2,1)}) custom-call(s32[4096]{0:T(1024)} %reshape.38.halo, s32[12288]{0:T(1024)} %reshape.39.pool_send, s32[4096]{0:T(1024)} %compare_select_fusion.senders, s32[4096]{0:T(1024)} %receivers.4, bf16[8192,128]{1,0:T(8,128)(2,1)} %nodes.1, bf16[4096,128]{1,0:T(8,128)(2,1)} %edges.2, ...), custom_call_target="tpu_custom_call" | custom-call | tf_op jit(solution)/shard_map/message_stage/pallas_call | solution.py:478
  60.8 12.8 %sum_stage.1 = bf16[12288,128]{1,0:T(8,128)(2,1)} custom-call(s32[4096]{0:T(1024)} %receivers.4, s32[8192]{0:T(1024)} %fusion.2.place.index, f32[4096,128]{1,0:T(8,128)} %get-tuple-element.6.msg), custom_call_target="tpu_custom_call" | custom-call | tf_op jit(solution)/shard_map/sum_stage/pallas_call | solution.py:108
  73.6 148.6 %main_stage.1 = (bf16[4,512,128]{2,1,0:T(8,128)(2,1)}, bf16[4,64,48,128]{3,2,1,0:T(8,128)(2,1)}) custom-call(s32[2048]{0:T(1024)} %reshape.34.halo, s32[3072]{0:T(1024)} %reshape.35.dest, s32[1024]{0:T(1024)} %compare_select_fusion.1.senders, s32[1024]{0:T(1024)} %receivers.5, s32[96,128]{1,0:T(8,128)} %reshape.36.all_dest, ...), custom_call_target="tpu_custom_call" | custom-call | tf_op jit(solution)/shard_map/main_stage/pallas_call | solution.py:685
  222.2 0.0 copy-start
  222.2 11.1 %final_stage.1 = bf16[8192,128]{1,0:T(8,128)(2,1)} custom-call(s32[8192]{0:T(1024)} %fusion.2.place.index, bf16[12288,128]{1,0:T(8,128)(2,1)} %bitcast.5), custom_call_target="tpu_custom_call" | custom-call | tf_op jit(solution)/shard_map/final_stage/pallas_call | solution.py:130
  233.3 0.0 copy-done
  233.3 0.8 copy.22
Async XLA Ops:
  222.2 11.1 %copy-start = (bf16[4,512,128]{2,1,0:T(8,128)(2,1)S(1)}, bf16[4,512,128]{2,1,0:T(8,128)(2,1)}, u32[]{:S(2)}) copy-start(bf16[4,512,128]{2,1,0:T(8,128)(2,1)} %get-tuple-element.9) | copy-start | bytes 1572868

commit v2 on v1

--- a/solution.py
+++ b/solution.py
@@ -10,6 +10,7 @@
 F32, BF16 = jnp.float32, jnp.bfloat16
 VMEM = pl.BlockSpec(memory_space=pltpu.VMEM)
 SMEM = pl.BlockSpec(memory_space=pltpu.SMEM)
+ANY = pl.BlockSpec(memory_space=pl.ANY)
 LANES = 128
 
 
@@ -98,21 +99,92 @@
     row_loop(msg.shape[0], step, body)
 
 
-def sum_kernel(receivers, place, msg, out, *accs):
+def sum_kernel(receivers, place, msg, out, held, total, sem_in, sem_out, *accs):
+    load = pltpu.make_async_copy(msg, held, sem_in)
+    load.start()
     clear_all(accs)
-    add_rows(lambda j: place[receivers[j]], msg, msg.shape[0], accs)
-    sum_accs(accs, out)
+    load.wait()
+    add_rows(lambda j: place[receivers[j]], held, held.shape[0], accs)
+    size = out.shape[0] // 4
+
+    def store(q):
+        at = pl.ds(q * size, size)
+        return pltpu.make_async_copy(total.at[at], out.at[at], sem_out.at[q])
+
+    for q in range(4):
+        at = pl.ds(q * size, size)
+        sum_accs([acc.at[at] for acc in accs], total.at[at])
+        store(q).start()
+    for q in range(4):
+        store(q).wait()
 
 
 def sum_stage(receivers, place, msg, slots):
     return pl.pallas_call(
         sum_kernel,
         out_shape=jax.ShapeDtypeStruct((slots, LANES), BF16),
-        in_specs=[SMEM, SMEM, VMEM],
-        out_specs=VMEM,
-        scratch_shapes=[pltpu.VMEM((slots, LANES), F32)] * 3,
+        in_specs=[SMEM, SMEM, ANY],
+        out_specs=ANY,
+        scratch_shapes=[
+            pltpu.VMEM(msg.shape, F32),
+            pltpu.VMEM((slots, LANES), BF16),
+            pltpu.SemaphoreType.DMA,
+            pltpu.SemaphoreType.DMA((4,)),
+        ]
+        + [pltpu.VMEM((slots, LANES), F32)] * 3,
         name="sum_stage",
     )(receivers, place, msg)
+
+
+def place_kernel(groups, widths, senders, far_senders, slots, out, far_out, place):
+    me = lax.axis_index("dom")
+    doms, rows, width, coarse_rows, coarse_width, slot_count = widths
+    per = doms // groups
+
+    def over(value, divisor):
+        shift = (divisor & -divisor).bit_length() - 1
+        left = divisor >> shift
+        value = lax.shift_right_logical(value, shift)
+        if left == 1:
+            return value
+        return lax.shift_right_logical(value * ((1 << 16) // left + 1), 16)
+
+    def split(value, divisor):
+        high = over(value, divisor)
+        return high, value - high * divisor
+
+    def nearby(p):
+        group, local = split(p, per)
+        away = me // per + groups - group
+        away = jnp.where(away >= groups, away - groups, away)
+        step = jnp.where(2 * away <= groups, jnp.maximum(2 * away - 1, 0), 2 * (groups - away))
+        return step * per + local
+
+    def moved(value, near, wide):
+        size = wide // 4
+        owner, slot = split(jnp.maximum(value - near, 0), wide)
+        quarter, inner = split(slot, size)
+        there = near + quarter * (doms * size) + nearby(owner) * size + inner
+        return jnp.where(value < near, value, there)
+
+    out[...] = moved(senders[...], rows, width)
+    far_out[...] = moved(far_senders[...], coarse_rows, coarse_width)
+    owner, slot = split(slots[...], slot_count)
+    size = slot_count // 4
+    quarter, inner = split(slot, size)
+    place[...] = quarter * (doms * size) + nearby(owner) * size + inner
+
+
+def place_stage(groups, widths, *ints):
+    shaped = [x.reshape(-1, LANES) for x in ints]
+    results = pl.pallas_call(
+        functools.partial(place_kernel, groups, widths),
+        out_shape=[jax.ShapeDtypeStruct(x.shape, jnp.int32) for x in shaped],
+        in_specs=[VMEM] * 3,
+        out_specs=[VMEM] * 3,
+        name="place_stage",
+    )(*shaped)
+    return [x.reshape(-1) for x in results]
 
 
 def final_kernel(index, table, out, wide, rows):
@@ -286,6 +358,7 @@
                 self.second(s - 1)
             work(s)
         self.second(self.pieces - 1)
+        work(self.pieces)
         for s in range(self.pieces):
             self.finish(s)
 
@@ -357,14 +430,12 @@
         for copy in (self.raw_right(c), self.raw_left(c), self.sum_right(c), self.sum_left(c)):
             copy.wait()
 
-    def run(self, use=lambda c: None, aside=lambda: None):
+    def run(self, use=lambda c: None):
         order = list(reversed(range(self.chunks)))
         self.start(order[0])
         for k, c in enumerate(order):
             if k + 1 < self.chunks:
                 self.start(order[k + 1])
-            if k == 0:
-                aside()
             self.through(c)
             if k:
                 self.finish(order[k - 1])
@@ -395,9 +466,9 @@
 
     def body(i, carry):
         k = blocks[0] + i
-        start, at = base(k), pl.multiple_of(k * size, size)
+        (line, start), at = base(k), pl.multiple_of(k * size, size)
         for j in range(size):
-            rows[pl.ds(at + j, 1), :] = table[pl.ds(index[start + j], 1), :]
+            rows[pl.ds(at + j, 1), :] = table[pl.ds(index[line, start + j], 1), :]
         dst[k] = rows[pl.ds(at, size), :].astype(BF16)
         return carry
 
@@ -413,7 +484,7 @@
     net = Net(doms, groups)
     net.greet()
     widen(nodes, wide)
-    gather_blocks(halo, lambda k: k * (4 * size) + net.e * size, wide, rows, send, (0, doms))
+    gather_blocks(halo, lambda k: (k, net.e * size), wide, rows, send, (0, doms))
     net.meet()
     land = ghosts.at[net.e]
     exchange = Exchange(
@@ -434,6 +505,7 @@
             msg[pl.ds(at + j, 1), :] = msg[pl.ds(at + j, 1), :] + table_r[pl.ds(receivers[at + j], 1), :]
 
     row_loop(count, 32, gather_near)
+    premultiply(nodes, w[0:LANES, :], table_s)
     each = groups // pieces
 
     def ready(s):
@@ -447,12 +519,13 @@
 
     def base(k):
         p = net.behind(k // net.per) + lax.rem(k, net.per)
-        return p * (4 * own_size) + net.e * own_size
+        return p, net.e * own_size
+
+    part = doms // (pieces + 1) if doms % (pieces + 1) == 0 else doms // (2 * pieces)
 
     def work(s):
-        gather_blocks(pool_send, base, wide, rows, own_nodes, (s * (doms // pieces), doms // pieces))
-        if s == pieces - 1:
-            premultiply(nodes, w[0:LANES, :], table_s)
+        first = s * part
+        gather_blocks(pool_send, base, wide, rows, own_nodes, (first, part if s < pieces else doms - first))
 
     Relay(net, ghosts, (r0, r1), pieces).run(ready, work)
     for owner in range(4):
@@ -473,7 +546,7 @@
 
 
 def message_stage(doms, groups, halo, pool_send, senders, receivers, nodes, edges, w_in, w_out, gain, pieces=2):
-    size, own_size = halo.shape[0] // doms // 4, pool_send.shape[0] // doms // 4
+    size, own_size = halo.shape[1] // 4, pool_send.shape[1] // 4
     near, count = nodes.shape[0], edges.shape[0]
     return pl.pallas_call(
         functools.partial(message_kernel, groups, pieces),
@@ -500,18 +573,18 @@
 
 
 def child_counts(all_dest, first, counts, step=128):
-    lines = all_dest.shape[0]
+    lines, width = all_dest.shape
 
     def rows(at):
-        target = lax.broadcasted_iota(jnp.int32, (step, LANES), 0) + (first + at)
+        target = lax.broadcasted_iota(jnp.int32, (step, width), 0) + (first + at)
 
         def line(i, total):
-            for j in range(8):
-                hit = all_dest[pl.ds(i * 8 + j, 1), :] == target
+            for j in range(4):
+                hit = all_dest[pl.ds(i * 4 + j, 1), :] == target
                 total = total + jnp.where(hit, 1.0, 0.0)
             return total
 
-        total = lax.fori_loop(0, lines // 8, line, jnp.zeros((step, LANES), F32))
+        total = lax.fori_loop(0, lines // 4, line, jnp.zeros((step, width), F32))
         counts[pl.ds(at, step), :] = jnp.broadcast_to(jnp.sum(total, axis=1, keepdims=True), (step, LANES))
 
     row_loop(counts.shape[0], step, rows)
@@ -524,9 +597,9 @@
 
 def main_kernel(
     groups, pieces, halo, dest, senders, receivers, all_dest, group_dest, line_receivers,
-    part, nodes, edges, edge_in, edge_out, node_in, node_out, edge_gain, node_gain,
+    part_there, nodes_there, edges, edge_in, edge_out, node_in, node_out, edge_gain, node_gain,
     coarse_out, table,
-    hop, passed, near, mid, arrived, counts, pooled, coarse_part, coarse_hop, coarse_passed, coarse_near,
+    part, nodes, load_sems, hop, passed, near, mid, arrived, counts, pooled, coarse_part, coarse_hop, coarse_passed, coarse_near,
     coarse_in, ghosts, wide, rows, border, table_s, table_r, msg, send, land,
     f0, f1, p0, p1, e0, e1, a0, a1, b0, b1, g0, g1, h0, h1, i0, i1, i2, j0, j1, j2, k0, k1, k2,
 ):
@@ -534,8 +607,16 @@
     quarter, border_size = coarse_in.shape[1], ghosts.shape[2]
     coarse_rows, count = 4 * quarter, edges.shape[0]
     net = Net(doms, groups)
+    load_part = pltpu.make_async_copy(part_there, part, load_sems.at[0])
+    load_nodes = pltpu.make_async_copy(nodes_there, nodes, load_sems.at[1])
+    load_part.start()
+    load_nodes.start()
     net.greet()
     premultiply(edges, edge_in[1, 2 * LANES :, :], msg)
+    child_counts(all_dest, net.e * quarter, counts)
+    pooled[...] = jnp.zeros_like(pooled)
+    load_part.wait()
+    load_nodes.wait()
     net.meet()
 
     reduce = Reduce(net, part, hop, passed, near, (f0, f1), groups // 2)
@@ -559,11 +640,7 @@
         for u in units:
             pool.send(u)
 
-    def aside():
-        pooled[...] = jnp.zeros_like(pooled)
-        child_counts(all_dest, net.e * quarter, counts)
-
-    reduce.run(use, aside)
+    reduce.run(use)
 
     def gathered(k, carry):
         c = groups // 2 - 1 - k // 2
@@ -595,7 +672,7 @@
     Relay(net, coarse_in, (g0, g1), 1).run()
     for q in range(4):
         wide[pl.ds(q * quarter, quarter), :] = coarse_in[q].astype(F32)
-    gather_blocks(halo, lambda k: k * (4 * border_size) + net.e * border_size, wide, rows, border, (0, doms))
+    gather_blocks(halo, lambda k: (k, net.e * border_size), wide, rows, border, (0, doms))
     here = ghosts.at[net.e]
     exchange = Exchange(
         net, net.ahead,
@@ -616,9 +693,18 @@
             msg[pl.ds(at + j, 1), :] = msg[pl.ds(at + j, 1), :] + table_r[pl.ds(receivers[at + j], 1), :]
 
     row_loop(count, 32, gather_near)
-    exchange.loop(exchange.receive)
-    exchange.finish()
-    Relay(net, ghosts, (h0, h1), 1).run()
+
+    def ready(s):
+        def run(t, carry):
+            exchange.receive(t)
+            return carry
+
+        lax.fori_loop(s * (groups // 2), (s + 1) * (groups // 2), run, 0)
+        if s == 0:
+            exchange.own().wait()
+
+    Relay(net, ghosts, (h0, h1), 2).run(ready)
+    exchange.loop(lambda t: exchange.each(t, lambda i: exchange.copy(t, i).wait_send()))
     for owner in range(4):
         block = ghosts[owner].reshape(doms * border_size, LANES)
         at = pl.ds(coarse_rows + owner * doms * border_size, doms * border_size)
@@ -655,7 +741,7 @@
     )
 
     def start(t):
-        gather_blocks(dest, lambda k: k * size, wide, rows, send, (net.ahead(t), net.per))
+        gather_blocks(dest, lambda k: (k, net.e * size), wide, rows, send, (net.ahead(t), net.per))
         back.send(t)
 
     back.loop(start)
@@ -680,7 +766,7 @@
 def main_stage(groups, coarse_rows, ints, part, nodes, edges, weights, pieces=4):
     doms, size, _ = nodes.shape
     pieces, quarter = min(pieces, groups), coarse_rows // 4
-    border_size, count = ints[0].shape[0] // doms // 4, edges.shape[0]
+    border_size, count = ints[0].shape[1] // 4, edges.shape[0]
     vmem = pltpu.VMEM
     return pl.pallas_call(
         functools.partial(main_kernel, groups, pieces),
@@ -688,9 +774,10 @@
             jax.ShapeDtypeStruct((4, quarter, LANES), BF16),
             jax.ShapeDtypeStruct((4,) + nodes.shape, BF16),
         ),
-        in_specs=[SMEM] * 4 + [VMEM] * 12,
+        in_specs=[SMEM] * 4 + [VMEM] * 3 + [ANY] * 2 + [VMEM] * 7,
         out_specs=(VMEM, VMEM),
-        scratch_shapes=reduce_scratch(part.shape[1], 1)[:3]
+        scratch_shapes=[vmem(part.shape, BF16), vmem(nodes.shape, BF16), pltpu.SemaphoreType.DMA((2,))]
+        + reduce_scratch(part.shape[1], 1)[:3]
         + [
             vmem(nodes.shape, BF16),
             vmem(nodes.shape, BF16),
@@ -717,7 +804,7 @@
         + relay_sems(1)
         + relay_sems(pieces)
         + relay_sems(1)
-        + relay_sems(1)
+        + relay_sems(2)
         + exchange_sems(doms)
         + exchange_sems(doms)
         + exchange_sems(doms),
@@ -733,38 +820,21 @@
         pool_send, pool_dest, unpool_slot,
         edge_in_weight, edge_out_weight, node_in_weight, node_out_weight, edge_gain, node_gain,
     ) = args
-    e, me = lax.axis_index("edge"), lax.axis_index("dom")
+    e = lax.axis_index("edge")
     doms = fine_halo.shape[1]
-    per = doms // groups
-
-    def nearby(p):
-        away = lax.rem(me // per + groups - p // per, groups)
-        step = jnp.where(2 * away <= groups, jnp.maximum(2 * away - 1, 0), 2 * (groups - away))
-        return step * per + lax.rem(p, per)
-
-    def moved(senders, rows, width):
-        far = senders - rows
-        size = width // 4
-        owner, slot = far // width, lax.rem(far, width)
-        there = rows + (slot // size) * (doms * size) + nearby(owner) * size + lax.rem(slot, size)
-        return jnp.where(senders < rows, senders, there)
-
     slots = pool_dest.shape[2]
-    own_size = slots // 4
-    slot = lax.rem(unpool_slot, slots)
-    place = (slot // own_size) * (doms * own_size) + nearby(unpool_slot // slots) * own_size + lax.rem(slot, own_size)
-    dest = lax.dynamic_slice_in_dim(pool_dest[0], e * own_size, own_size, axis=1).reshape(-1)
-    senders = moved(fine_senders, fine_nodes.shape[0], fine_halo.shape[2])
-    far_senders = moved(coarse_senders, coarse_rows, coarse_halo.shape[2])
+    group_dest = lax.dynamic_slice_in_dim(pool_dest[0], e * (slots // 4), slots // 4, axis=1).reshape(groups, -1)
+    widths = (doms, fine_nodes.shape[0], fine_halo.shape[2], coarse_rows, coarse_halo.shape[2], slots)
+    senders, far_senders, place = place_stage(groups, widths, fine_senders, coarse_senders, unpool_slot)
 
     msg, own_nodes = message_stage(
-        doms, groups, fine_halo.reshape(-1), pool_send.reshape(-1), senders, fine_receivers,
+        doms, groups, fine_halo[0], pool_send[0], senders, fine_receivers,
         fine_nodes, fine_edges, edge_in_weight, edge_out_weight, edge_gain,
     )
     part = sum_stage(fine_receivers, place, msg, doms * slots)
     ints = (
-        coarse_halo.reshape(-1), dest, far_senders, coarse_receivers,
-        pool_dest.reshape(-1, LANES), dest.reshape(groups, -1), coarse_receivers.reshape(1, -1),
+        coarse_halo[0], pool_dest[0], far_senders, coarse_receivers,
+        pool_dest[0], group_dest, coarse_receivers.reshape(1, -1),
     )
     weights = (edge_in_weight, edge_out_weight, node_in_weight, node_out_weight, edge_gain, node_gain)
     coarse_out, table = main_stage(

time: 236 us -> 231 us (0.979)
  Pallas kernels: 220 us -> 226 us
  local copies, waits for them, and re-layouts: 9.05 us -> 3.81 us
  other arithmetic: 4.14 us -> 0 us
    reshape x5 -> x1, local copies, waits for them, and re-layouts: 5.86 us -> 0.68 us  [shards(): lax.dynamic_slice_in_dim(pool_dest[0], e * (slots // 4), slots // 4, axis=1)]
    pallas_call x1, Pallas kernels: 47.8 us -> 51.4 us  [message_stage(): pl.pallas_call(functools.partial(message_kernel, groups, pieces), out_sha...]
    select_n x2 -> x0, other arithmetic: 2.68 us -> none  [moved(): return jnp.where(senders < rows, senders, there)]
where the time goes in v2:
time: 231 us
  Pallas kernels  226 us (98%)
  local copies, waits for them, and re-layouts  3.81 us (2%)
    pallas_call x1, Pallas kernels, main_stage(): pl.pallas_call(functools.partial(main_kernel, groups, pieces), out_shape=...  150 us
    pallas_call x1, Pallas kernels, message_stage(): pl.pallas_call(functools.partial(message_kernel, groups, pieces), out_sha...  51.4 us
    pallas_call x1, Pallas kernels, sum_stage(): pl.pallas_call(sum_kernel, out_shape=jax.ShapeDtypeStruct((slots, LANES),...  12.3 us
    pallas_call x1, Pallas kernels, final_stage(): pl.pallas_call(final_kernel, out_shape=jax.ShapeDtypeStruct((count, LANES...  11.1 us

profile of v2, /device:TPU:1, one launch (start us, length us, event | category | flops | bytes accessed | tf_op | source)
XLA Modules:
  0.0 230.9 jit_solution(3791462135994603497)
XLA Ops:
  0.6 0.9 constant_dynamic-slice_fusion
  1.6 0.7 reshape.44.group_dest
  2.2 1.4 copy.21
  3.6 1.5 place_stage.1
  5.1 51.4 %message_stage.1 = (f32[4096,128]{1,0:T(8,128)}, bf16[64,48,128]{2,1,0:T(8,128)(2,1)}) custom-call(s32[64,64]{1,0:T(8,128)} %bitcast.24, s32[64,192]{1,0:T(8,128)} %bitcast.22, s32[4096]{0:T(1024)} %bitcast.25, s32[4096]{0:T(1024)} %receivers.4, bf16[8192,128]{1,0:T(8,128)(2,1)} %nodes.1, bf16[4096,128]{1,0:T(8,128)(2,1)} %edges.2, ...), custom_call_target="tpu_custom_call" | custom-call | tf_op jit(solution)/shard_map/message_stage/pallas_call | solution.py:551
  56.6 12.3 %sum_stage.1 = bf16[12288,128]{1,0:T(8,128)(2,1)} custom-call(s32[4096]{0:T(1024)} %receivers.4, s32[8192]{0:T(1024)} %bitcast.19, f32[4096,128]{1,0:T(8,128)} %get-tuple-element.12.msg), custom_call_target="tpu_custom_call" | custom-call | tf_op jit(solution)/shard_map/sum_stage/pallas_call | solution.py:123
  68.9 150.1 %main_stage.1 = (bf16[4,512,128]{2,1,0:T(8,128)(2,1)}, bf16[4,64,48,128]{3,2,1,0:T(8,128)(2,1)}) custom-call(s32[64,32]{1,0:T(8,128)} %bitcast.21, s32[64,192]{1,0:T(8,128)} %bitcast.17, s32[1024]{0:T(1024)} %bitcast.29, s32[1024]{0:T(1024)} %receivers.5, s32[64,192]{1,0:T(8,128)} %bitcast.18, s32[8,384]{1,0:T(8,128)} %reshape.44.group_dest, ...), custom_call_target="tpu_custom_call" | custom-call | tf_op jit(solution)/shard_map/main_stage/pallas_call | solution.py:771
  219.0 0.0 copy-start
  219.0 11.1 %final_stage.1 = bf16[8192,128]{1,0:T(8,128)(2,1)} custom-call(s32[8192]{0:T(1024)} %bitcast.20, bf16[12288,128]{1,0:T(8,128)(2,1)} %bitcast.15), custom_call_target="tpu_custom_call" | custom-call | tf_op jit(solution)/shard_map/final_stage/pallas_call | solution.py:202
  230.1 0.0 copy-done
  230.1 0.8 copy.23
Async XLA Ops:
  219.0 11.1 %copy-start = (bf16[4,512,128]{2,1,0:T(8,128)(2,1)S(1)}, bf16[4,512,128]{2,1,0:T(8,128)(2,1)}, u32[]{:S(2)}) copy-start(bf16[4,512,128]{2,1,0:T(8,128)(2,1)} %get-tuple-element.15) | copy-start | bytes 1572868

commit v3 on v2

--- a/solution.py
+++ b/solution.py
@@ -47,14 +47,6 @@
         dst[pl.ds(at, step), :] = src[pl.ds(at, step), :].astype(F32)
 
     row_loop(src.shape[0], step, body)
-
-
-def gather_rows(index, table, dst, count, unroll=16):
-    def body(at):
-        for j in range(unroll):
-            dst[pl.ds(at + j, 1), :] = table[pl.ds(index[at + j], 1), :]
-
-    row_loop(count, unroll, body)
 
 
 def clear_all(accs, step=512):
@@ -187,28 +179,6 @@
     return [x.reshape(-1) for x in results]
 
 
-def final_kernel(index, table, out, wide, rows):
-    widen(table, wide)
-    gather_rows(index, wide, rows, out.shape[0], 64)
-
-    def pack(at):
-        out[pl.ds(at, 512), :] = rows[pl.ds(at, 512), :].astype(BF16)
-
-    row_loop(out.shape[0], 512, pack)
-
-
-def final_stage(index, table):
-    count = index.shape[0]
-    return pl.pallas_call(
-        final_kernel,
-        out_shape=jax.ShapeDtypeStruct((count, LANES), BF16),
-        in_specs=[SMEM, VMEM],
-        out_specs=VMEM,
-        scratch_shapes=[pltpu.VMEM(table.shape, F32), pltpu.VMEM((count, LANES), F32)],
-        name="final_stage",
-    )(index, table)
-
-
 class Net:
     def __init__(self, doms, groups):
         self.doms, self.groups, self.per = doms, groups, doms // groups
@@ -317,15 +287,19 @@
 
 
 class Relay:
-    def __init__(self, net, out, sems, pieces):
-        self.net, self.out, self.sems, self.pieces = net, out, sems, pieces
-        self.size = out.shape[1] // pieces
+    def __init__(self, net, out, sems, sizes):
+        self.net, self.out, self.sems, self.sizes = net, out, sems, sizes
+        self.pieces = len(sizes)
+
+    def range(self, s):
+        return sum(self.sizes[:s]), self.sizes[s]
 
     def copy(self, which, owner, s, half, to):
+        first, size = self.range(s)
         if half is None:
-            at = pl.ds(s * self.size, self.size)
+            at = pl.ds(first, size)
         else:
-            at = pl.ds(s * self.size + half * (self.size // 2), self.size // 2)
+            at = pl.ds(first + half * (size // 2), size // 2)
         piece = self.out.at[owner, at]
         return edge_copy(piece, piece, self.sems, which, s, to)
 
@@ -350,17 +324,23 @@
         self.copy(2, n.left, s, 0, n.right).wait_send()
         self.copy(3, n.right, s, 1, n.left).wait_send()
 
-    def run(self, ready=lambda s: None, work=lambda s: None):
-        for s in range(self.pieces):
-            ready(s)
-            self.first(s)
+    def run(self, ready=lambda s: None, work=lambda s: None, got=lambda owner, s: None):
+        n, last = self.net, self.pieces - 1
+        for s in range(self.pieces + 1):
+            if s <= last:
+                ready(s)
+                self.first(s)
             if s:
                 self.second(s - 1)
             work(s)
-        self.second(self.pieces - 1)
-        work(self.pieces)
+            if s <= last:
+                got(n.e, s)
+            if s:
+                got(n.left, s - 1)
+                got(n.right, s - 1)
         for s in range(self.pieces):
             self.finish(s)
+            got(n.opp, s)
 
 
 def relay_sems(pieces):
@@ -466,9 +446,9 @@
 
     def body(i, carry):
         k = blocks[0] + i
-        (line, start), at = base(k), pl.multiple_of(k * size, size)
+        line, at = base(k), pl.multiple_of(k * size, size)
         for j in range(size):
-            rows[pl.ds(at + j, 1), :] = table[pl.ds(index[line, start + j], 1), :]
+            rows[pl.ds(at + j, 1), :] = table[pl.ds(index[line, j], 1), :]
         dst[k] = rows[pl.ds(at, size), :].astype(BF16)
         return carry
 
@@ -484,7 +464,7 @@
     net = Net(doms, groups)
     net.greet()
     widen(nodes, wide)
-    gather_blocks(halo, lambda k: (k, net.e * size), wide, rows, send, (0, doms))
+    gather_blocks(halo, lambda k: k, wide, rows, send, (0, doms))
     net.meet()
     land = ghosts.at[net.e]
     exchange = Exchange(
@@ -519,7 +499,7 @@
 
     def base(k):
         p = net.behind(k // net.per) + lax.rem(k, net.per)
-        return p, net.e * own_size
+        return p
 
     part = doms // (pieces + 1) if doms % (pieces + 1) == 0 else doms // (2 * pieces)
 
@@ -527,7 +507,7 @@
         first = s * part
         gather_blocks(pool_send, base, wide, rows, own_nodes, (first, part if s < pieces else doms - first))
 
-    Relay(net, ghosts, (r0, r1), pieces).run(ready, work)
+    Relay(net, ghosts, (r0, r1), [doms // pieces] * pieces).run(ready, work)
     for owner in range(4):
         block = ghosts[owner].reshape(doms * size, LANES)
         table_s[pl.ds(near + owner * doms * size, doms * size), :] = dot(block, w[0:LANES, :])
@@ -546,7 +526,7 @@
 
 
 def message_stage(doms, groups, halo, pool_send, senders, receivers, nodes, edges, w_in, w_out, gain, pieces=2):
-    size, own_size = halo.shape[1] // 4, pool_send.shape[1] // 4
+    size, own_size = halo.shape[1], pool_send.shape[1]
     near, count = nodes.shape[0], edges.shape[0]
     return pl.pallas_call(
         functools.partial(message_kernel, groups, pieces),
@@ -596,10 +576,10 @@
 
 
 def main_kernel(
-    groups, pieces, halo, dest, senders, receivers, all_dest, group_dest, line_receivers,
+    groups, pieces, halo, dest, senders, receivers, place, all_dest, group_dest, line_receivers,
     part_there, nodes_there, edges, edge_in, edge_out, node_in, node_out, edge_gain, node_gain,
-    coarse_out, table,
-    part, nodes, load_sems, hop, passed, near, mid, arrived, counts, pooled, coarse_part, coarse_hop, coarse_passed, coarse_near,
+    coarse_out, fine_out,
+    table, fine_wide, part, nodes, load_sems, hop, passed, near, mid, arrived, counts, pooled, coarse_part, coarse_hop, coarse_passed, coarse_near,
     coarse_in, ghosts, wide, rows, border, table_s, table_r, msg, send, land,
     f0, f1, p0, p1, e0, e1, a0, a1, b0, b1, g0, g1, h0, h1, i0, i1, i2, j0, j1, j2, k0, k1, k2,
 ):
@@ -665,14 +645,18 @@
         coarse_part[owner] = pooled[at, :].astype(BF16)
     pool.loop(lambda t: pool.each(t, lambda i: pool.copy(t, i).wait_send()))
 
+    def spread(values):
+        def got(owner, s):
+            wide[pl.ds(pl.multiple_of(owner * quarter, quarter), quarter), :] = values[owner].astype(F32)
+
+        return got
+
     reduce = Reduce(net, coarse_part, coarse_hop, coarse_passed, coarse_near, (p0, p1), p0.shape[1])
     reduce.run()
     mean = reduce.value(pl.ds(0, quarter)) / jnp.maximum(counts[...], 1.0)
     coarse_in[net.e] = mean.astype(BF16)
-    Relay(net, coarse_in, (g0, g1), 1).run()
-    for q in range(4):
-        wide[pl.ds(q * quarter, quarter), :] = coarse_in[q].astype(F32)
-    gather_blocks(halo, lambda k: (k, net.e * border_size), wide, rows, border, (0, doms))
+    Relay(net, coarse_in, (g0, g1), [quarter]).run(got=spread(coarse_in))
+    gather_blocks(halo, lambda k: k, wide, rows, border, (0, doms))
     here = ghosts.at[net.e]
     exchange = Exchange(
         net, net.ahead,
@@ -703,7 +687,7 @@
         if s == 0:
             exchange.own().wait()
 
-    Relay(net, ghosts, (h0, h1), 2).run(ready)
+    Relay(net, ghosts, (h0, h1), [doms // 2] * 2).run(ready)
     exchange.loop(lambda t: exchange.each(t, lambda i: exchange.copy(t, i).wait_send()))
     for owner in range(4):
         block = ghosts[owner].reshape(doms * border_size, LANES)
@@ -729,9 +713,7 @@
         coarse_in[net.e], reduce.value(pl.ds(0, quarter)), node_in[1], node_out[1], node_gain[1:2, :]
     )
     wide[pl.ds(coarse_rows, 8), :] = jnp.zeros((8, LANES), F32)
-    Relay(net, coarse_out, (a0, a1), 1).run()
-    for q in range(4):
-        wide[pl.ds(q * quarter, quarter), :] = coarse_out[q].astype(F32)
+    Relay(net, coarse_out, (a0, a1), [quarter]).run(got=spread(coarse_out))
     back = Exchange(
         net, net.ahead,
         lambda t, peer: send.at[peer],
@@ -741,42 +723,64 @@
     )
 
     def start(t):
-        gather_blocks(dest, lambda k: (k, net.e * size), wide, rows, send, (net.ahead(t), net.per))
+        gather_blocks(dest, lambda k: k, wide, rows, send, (net.ahead(t), net.per))
         back.send(t)
 
     back.loop(start)
     back.own().start()
-    each = groups // pieces
+    ends = [sum(pieces[:s]) for s in range(len(pieces) + 1)]
 
     def ready(s):
         def run(t, carry):
             back.receive(t)
             return carry
 
-        lax.fori_loop(s * each, (s + 1) * each, run, 0)
+        lax.fori_loop(ends[s], ends[s + 1], run, 0)
         if s == 0:
             back.own().wait()
-        block = slice(s * each * net.per, (s + 1) * each * net.per)
+        block = slice(ends[s] * net.per, ends[s + 1] * net.per)
         table[net.e, block] = (land[block].astype(F32) + mid[block].astype(F32)).astype(BF16)
 
-    Relay(net, table, (b0, b1), pieces).run(ready)
+    relay = Relay(net, table, (b0, b1), [p * net.per for p in pieces])
+
+    def got(owner, s):
+        first, count = relay.range(s)
+        at = pl.multiple_of(owner * (doms * size) + first * size, 16)
+        block = table[owner, pl.ds(first, count)].reshape(count * size, LANES)
+        fine_wide[pl.ds(at, count * size), :] = block.astype(F32)
+
+    relay.run(ready, got=got)
+
+    def pick(at):
+        for half in (0, 64):
+            for j in range(half, half + 64):
+                rows[pl.ds(j, 1), :] = fine_wide[pl.ds(place[at + j], 1), :]
+            fine_out[pl.ds(at + half, 64), :] = rows[half : half + 64, :].astype(BF16)
+
+    row_loop(fine_out.shape[0], 128, pick)
     back.loop(lambda t: back.each(t, lambda i: back.copy(t, i).wait_send()))
 
 
-def main_stage(groups, coarse_rows, ints, part, nodes, edges, weights, pieces=4):
+def main_stage(groups, coarse_rows, ints, part, nodes, edges, weights, fine_rows, pieces=(2, 2, 2, 1, 1)):
     doms, size, _ = nodes.shape
-    pieces, quarter = min(pieces, groups), coarse_rows // 4
-    border_size, count = ints[0].shape[1] // 4, edges.shape[0]
+    quarter = coarse_rows // 4
+    border_size, count = ints[0].shape[1], edges.shape[0]
     vmem = pltpu.VMEM
     return pl.pallas_call(
         functools.partial(main_kernel, groups, pieces),
         out_shape=(
             jax.ShapeDtypeStruct((4, quarter, LANES), BF16),
-            jax.ShapeDtypeStruct((4,) + nodes.shape, BF16),
+            jax.ShapeDtypeStruct((fine_rows, LANES), BF16),
         ),
-        in_specs=[SMEM] * 4 + [VMEM] * 3 + [ANY] * 2 + [VMEM] * 7,
+        in_specs=[SMEM] * 5 + [VMEM] * 3 + [ANY] * 2 + [VMEM] * 7,
         out_specs=(VMEM, VMEM),
-        scratch_shapes=[vmem(part.shape, BF16), vmem(nodes.shape, BF16), pltpu.SemaphoreType.DMA((2,))]
+        scratch_shapes=[
+            vmem((4,) + nodes.shape, BF16),
+            vmem((4 * doms * size, LANES), F32),
+            vmem(part.shape, BF16),
+            vmem(nodes.shape, BF16),
+            pltpu.SemaphoreType.DMA((2,)),
+        ]
         + reduce_scratch(part.shape[1], 1)[:3]
         + [
             vmem(nodes.shape, BF16),
@@ -802,7 +806,7 @@
         + reduce_scratch(quarter, 2)[3:]
         + reduce_scratch(quarter, 2)[3:]
         + relay_sems(1)
-        + relay_sems(pieces)
+        + relay_sems(len(pieces))
         + relay_sems(1)
         + relay_sems(2)
         + exchange_sems(doms)
@@ -823,24 +827,29 @@
     e = lax.axis_index("edge")
     doms = fine_halo.shape[1]
     slots = pool_dest.shape[2]
-    group_dest = lax.dynamic_slice_in_dim(pool_dest[0], e * (slots // 4), slots // 4, axis=1).reshape(groups, -1)
+
+    def quarter(lists):
+        size = lists.shape[2] // 4
+        return lax.dynamic_slice_in_dim(lists[0], e * size, size, axis=1)
+
+    own, dest = quarter(pool_send), quarter(pool_dest)
+    group_dest = dest.reshape(groups, -1)
     widths = (doms, fine_nodes.shape[0], fine_halo.shape[2], coarse_rows, coarse_halo.shape[2], slots)
     senders, far_senders, place = place_stage(groups, widths, fine_senders, coarse_senders, unpool_slot)
 
     msg, own_nodes = message_stage(
-        doms, groups, fine_halo[0], pool_send[0], senders, fine_receivers,
+        doms, groups, quarter(fine_halo), own, senders, fine_receivers,
         fine_nodes, fine_edges, edge_in_weight, edge_out_weight, edge_gain,
     )
     part = sum_stage(fine_receivers, place, msg, doms * slots)
     ints = (
-        coarse_halo[0], pool_dest[0], far_senders, coarse_receivers,
+        quarter(coarse_halo), dest, far_senders, coarse_receivers, place,
         pool_dest[0], group_dest, coarse_receivers.reshape(1, -1),
     )
     weights = (edge_in_weight, edge_out_weight, node_in_weight, node_out_weight, edge_gain, node_gain)
-    coarse_out, table = main_stage(
-        groups, coarse_rows, ints, part.reshape(4, -1, LANES), own_nodes, coarse_edges, weights
-    )
-    fine_out = final_stage(place, table.reshape(-1, LANES))
+    coarse_out, fine_out = main_stage(
+        groups, coarse_rows, ints, part.reshape(4, -1, LANES), own_nodes, coarse_edges, weights, fine_nodes.shape[0]
+    )
     return fine_out, coarse_out.reshape(-1, LANES)
 
 

time: 231 us -> 231 us (level)
  Pallas kernels: 226 us -> 219 us
  local copies, waits for them, and re-layouts: 3.81 us -> 10.6 us
    pallas_call x1 -> x0, Pallas kernels: 11.1 us -> none  [final_stage(): pl.pallas_call(final_kernel, out_shape=jax.ShapeDtypeStruct((count, LANES...]
    pallas_call x1, Pallas kernels: 150 us -> 156 us  [main_stage(): pl.pallas_call(functools.partial(main_kernel, groups, pieces), out_shape=...]
    dynamic_slice x1 -> x6, local copies, waits for them, and re-layouts: 0.92 us -> 6.01 us  [quarter(): return lax.dynamic_slice_in_dim(lists[0], e * size, size, axis=1)]
    pallas_call x1, Pallas kernels: 51.4 us -> 48.3 us  [message_stage(): pl.pallas_call(functools.partial(message_kernel, groups, pieces), out_sha...]
where the time goes in v3:
time: 231 us; the launch traced here: 230 us
  Pallas kernels  219 us (95%)
  local copies, waits for them, and re-layouts  10.6 us (5%)
    pallas_call x1, Pallas kernels, main_stage(): pl.pallas_call(functools.partial(main_kernel, groups, pieces), out_shape=...  156 us
    pallas_call x1, Pallas kernels, message_stage(): pl.pallas_call(functools.partial(message_kernel, groups, pieces), out_sha...  48.3 us
    pallas_call x1, Pallas kernels, sum_stage(): pl.pallas_call(sum_kernel, out_shape=jax.ShapeDtypeStruct((slots, LANES),...  12.3 us
    dynamic_slice x6, local copies, waits for them, and re-layouts, quarter(): return lax.dynamic_slice_in_dim(lists[0], e * size, size, axis=1)  6.01 us

profile of v3, /device:TPU:1, one launch (start us, length us, event | category | flops | bytes accessed | tf_op | source)
XLA Modules:
  0.0 229.8 jit_solution(12834347647875703139)
XLA Ops:
  0.6 0.0 copy-start
  0.7 0.7 constant_dynamic-slice_fusion.1
  1.4 0.7 copy.21
  2.1 1.5 dynamic-slice_bitcast_fusion.1.halo
  3.5 0.0 copy-done
  3.5 0.7 dynamic-slice_bitcast_fusion.pool_send
  4.2 1.5 fusion.dest
  5.8 0.9 constant_dynamic-slice_fusion
  6.7 0.7 reshape.44.group_dest
  7.4 1.5 place_stage.1
  8.8 48.3 %message_stage.1 = (f32[4096,128]{1,0:T(8,128)}, bf16[64,48,128]{2,1,0:T(8,128)(2,1)}) custom-call(s32[64,16]{1,0:T(8,128)} %dynamic-slice_bitcast_fusion.1.halo, s32[64,48]{1,0:T(8,128)} %dynamic-slice_bitcast_fusion.pool_send, s32[4096]{0:T(1024)} %bitcast.24, s32[4096]{0:T(1024)} %receivers.4, bf16[8192,128]{1,0:T(8,128)(2,1)} %nodes.1, ...), custom_call_target="tpu_custom_call" | custom-call | tf_op jit(solution)/shard_map/message_stage/pallas_call | solution.py:531
  57.1 12.3 %sum_stage.1 = bf16[12288,128]{1,0:T(8,128)(2,1)} custom-call(s32[4096]{0:T(1024)} %receivers.4, s32[8192]{0:T(1024)} %bitcast.20, f32[4096,128]{1,0:T(8,128)} %get-tuple-element.12.msg), custom_call_target="tpu_custom_call" | custom-call | tf_op jit(solution)/shard_map/sum_stage/pallas_call | solution.py:115
  69.5 156.4 %main_stage.1 = (bf16[4,512,128]{2,1,0:T(8,128)(2,1)}, bf16[8192,128]{1,0:T(8,128)(2,1)}) custom-call(s32[64,8]{1,0:T(8,128)} %bitcast.22, s32[64,48]{1,0:T(8,128)} %fusion.dest, s32[1024]{0:T(1024)} %bitcast.28, s32[1024]{0:T(1024)} %receivers.5, s32[8192]{0:T(1024)} %bitcast.21, s32[64,192]{1,0:T(8,128)} %bitcast.19, s32[8,384]{1,0:T(8,128)} %reshape.44.group_dest, ...), custom_call_target="tpu_custom_call" | custom-call | tf_op jit(solution)/shard_map/main_stage/pallas_call | solution.py:769
  225.9 0.0 copy-start.1
  225.9 3.1 %copy.24 = bf16[8192,128]{1,0:T(8,128)(2,1)} copy(bf16[8192,128]{1,0:T(8,128)(2,1)} %get-tuple-element.18) | data formatting | bytes 4194304
  229.0 0.0 copy-done.1
  229.0 0.8 copy.25
Async XLA Ops:
  0.6 2.9 %copy-start = (s32[1,64,192]{2,1,0:T(8,128)S(1)}, s32[1,64,192]{2,1,0:T(8,128)}, u32[]{:S(2)}) copy-start(s32[1,64,192]{2,1,0:T(8,128)} %param.27) | copy-start | bytes 147460
  225.9 3.1 %copy-start.1 = (bf16[4,512,128]{2,1,0:T(8,128)(2,1)S(1)}, bf16[4,512,128]{2,1,0:T(8,128)(2,1)}, u32[]{:S(2)}) copy-start(bf16[4,512,128]{2,1,0:T(8,128)(2,1)} %get-tuple-element.15) | copy-start | bytes 1572868

commit v4 on v3

--- a/solution.py
+++ b/solution.py
@@ -128,7 +128,7 @@
     )(receivers, place, msg)
 
 
-def place_kernel(groups, widths, senders, far_senders, slots, out, far_out, place):
+def place_kernel(groups, widths, senders, far_senders, slots, lists, out, far_out, place, cuts):
     me = lax.axis_index("dom")
     doms, rows, width, coarse_rows, coarse_width, slot_count = widths
     per = doms // groups
@@ -166,17 +166,36 @@
     quarter, inner = split(slot, size)
     place[...] = quarter * (doms * size) + nearby(owner) * size + inner
 
-
-def place_stage(groups, widths, *ints):
+    e = lax.axis_index("edge")
+    for whole, cut in zip(lists, cuts):
+        axis = 0 if whole.shape[0] != cut.shape[0] else 1
+        size = cut.shape[axis]
+        pieces = [whole[q * size : (q + 1) * size] if axis == 0 else whole[:, q * size : (q + 1) * size] for q in range(4)]
+        value = pieces[3]
+        for q in range(3):
+            value = jnp.where(e == q, pieces[q], value)
+        cut[...] = value
+
+
+def place_stage(groups, widths, ints, lists):
     shaped = [x.reshape(-1, LANES) for x in ints]
+    cut_shapes = [
+        tuple(n // 4 if i == axis else n for i, n in enumerate(whole.shape)) for whole, axis in lists
+    ]
+    shapes = [x.shape for x in shaped] + cut_shapes
+
+    def kernel(*refs):
+        k = 3 + len(lists)
+        place_kernel(groups, widths, *refs[0:3], refs[3:k], *refs[k : k + 3], refs[k + 3 :])
+
     results = pl.pallas_call(
-        functools.partial(place_kernel, groups, widths),
-        out_shape=[jax.ShapeDtypeStruct(x.shape, jnp.int32) for x in shaped],
-        in_specs=[VMEM] * 3,
-        out_specs=[VMEM] * 3,
+        kernel,
+        out_shape=[jax.ShapeDtypeStruct(s, jnp.int32) for s in shapes],
+        in_specs=[VMEM] * len(shapes),
+        out_specs=[VMEM] * len(shapes),
         name="place_stage",
-    )(*shaped)
-    return [x.reshape(-1) for x in results]
+    )(*shaped, *(whole for whole, _ in lists))
+    return [x.reshape(-1) for x in results[:3]] + list(results[3:])
 
 
 class Net:
@@ -323,6 +342,18 @@
         self.copy(1, n.e, s, None, n.left).wait_send()
         self.copy(2, n.left, s, 0, n.right).wait_send()
         self.copy(3, n.right, s, 1, n.left).wait_send()
+
+    def rest(self, got):
+        n = self.net
+        for s in reversed(range(self.pieces)):
+            got(n.e, s)
+            self.second(s)
+        for s in reversed(range(self.pieces)):
+            got(n.left, s)
+            got(n.right, s)
+        for s in reversed(range(self.pieces)):
+            self.finish(s)
+            got(n.opp, s)
 
     def run(self, ready=lambda s: None, work=lambda s: None, got=lambda owner, s: None):
         n, last = self.net, self.pieces - 1
@@ -354,17 +385,20 @@
         self.half = part.shape[1] // 2
         self.size = self.half // chunks
 
+    def h(self, c):
+        return pl.ds(c * self.size, self.size)
+
     def a(self, c):
-        return pl.ds(pl.multiple_of(c * self.size, self.size), self.size)
+        return pl.ds(2 * c * self.size, self.size)
 
     def b(self, c):
-        return pl.ds(pl.multiple_of(self.half + c * self.size, self.size), self.size)
+        return pl.ds((2 * c + 1) * self.size, self.size)
 
     def hop_right(self, c):
-        return edge_copy(self.part.at[self.net.opp, self.a(c)], self.hop.at[0, self.a(c)], self.sems, 0, c, self.net.right)
+        return edge_copy(self.part.at[self.net.opp, self.a(c)], self.hop.at[0, self.h(c)], self.sems, 0, c, self.net.right)
 
     def hop_left(self, c):
-        return edge_copy(self.part.at[self.net.opp, self.b(c)], self.hop.at[1, self.a(c)], self.sems, 1, c, self.net.left)
+        return edge_copy(self.part.at[self.net.opp, self.b(c)], self.hop.at[1, self.h(c)], self.sems, 1, c, self.net.left)
 
     def raw_right(self, c):
         return edge_copy(self.part.at[self.net.right, self.b(c)], self.near.at[0, self.b(c)], self.sems, 2, c, self.net.right)
@@ -373,10 +407,10 @@
         return edge_copy(self.part.at[self.net.left, self.a(c)], self.near.at[1, self.a(c)], self.sems, 3, c, self.net.left)
 
     def sum_right(self, c):
-        return edge_copy(self.passed.at[0, self.a(c)], self.near.at[0, self.a(c)], self.sems, 4, c, self.net.right)
+        return edge_copy(self.passed.at[0, self.h(c)], self.near.at[0, self.a(c)], self.sems, 4, c, self.net.right)
 
     def sum_left(self, c):
-        return edge_copy(self.passed.at[1, self.a(c)], self.near.at[1, self.b(c)], self.sems, 5, c, self.net.left)
+        return edge_copy(self.passed.at[1, self.h(c)], self.near.at[1, self.b(c)], self.sems, 5, c, self.net.left)
 
     def loop(self, body):
         def run(c, carry):
@@ -394,12 +428,12 @@
     def through(self, c):
         net = self.net
         self.hop_right(c).wait_recv()
-        self.passed[0, self.a(c)] = (
-            self.hop[0, self.a(c)].astype(F32) + self.part[net.right, self.a(c)].astype(F32)
+        self.passed[0, self.h(c)] = (
+            self.hop[0, self.h(c)].astype(F32) + self.part[net.right, self.a(c)].astype(F32)
         ).astype(BF16)
         self.hop_left(c).wait_recv()
-        self.passed[1, self.a(c)] = (
-            self.hop[1, self.a(c)].astype(F32) + self.part[net.left, self.b(c)].astype(F32)
+        self.passed[1, self.h(c)] = (
+            self.hop[1, self.h(c)].astype(F32) + self.part[net.left, self.b(c)].astype(F32)
         ).astype(BF16)
         self.hop_right(c).wait_send()
         self.hop_left(c).wait_send()
@@ -410,12 +444,14 @@
         for copy in (self.raw_right(c), self.raw_left(c), self.sum_right(c), self.sum_left(c)):
             copy.wait()
 
-    def run(self, use=lambda c: None):
+    def run(self, use=lambda c: None, aside=lambda: None):
         order = list(reversed(range(self.chunks)))
         self.start(order[0])
         for k, c in enumerate(order):
             if k + 1 < self.chunks:
                 self.start(order[k + 1])
+            if k == 0:
+                aside()
             self.through(c)
             if k:
                 self.finish(order[k - 1])
@@ -441,14 +477,14 @@
     ]
 
 
-def gather_blocks(index, base, table, rows, dst, blocks):
+def gather_blocks(index, base, table, rows, dst, blocks, turned=False):
     size = dst.shape[1]
 
     def body(i, carry):
         k = blocks[0] + i
         line, at = base(k), pl.multiple_of(k * size, size)
         for j in range(size):
-            rows[pl.ds(at + j, 1), :] = table[pl.ds(index[line, j], 1), :]
+            rows[pl.ds(at + j, 1), :] = table[pl.ds(index[j, line] if turned else index[line, j], 1), :]
         dst[k] = rows[pl.ds(at, size), :].astype(BF16)
         return carry
 
@@ -456,10 +492,10 @@
 
 
 def message_kernel(
-    groups, pieces, halo, pool_send, senders, receivers, nodes, edges, w_in, w_out, gain,
-    out, own_nodes, ghosts, wide, rows, send, table_s, table_r, msg, s0, s1, s2, r0, r1,
+    groups, pieces, halo, senders, receivers, nodes, edges, w_in, w_out, gain,
+    out, ghosts, wide, rows, send, from_rows, to_rows, s0, s1, s2, r0, r1,
 ):
-    doms, size, own_size = ghosts.shape[1], ghosts.shape[2], own_nodes.shape[1]
+    doms, size = ghosts.shape[1], ghosts.shape[2]
     count, near = edges.shape[0], nodes.shape[0]
     net = Net(doms, groups)
     net.greet()
@@ -476,16 +512,23 @@
     )
     exchange.own().start()
     exchange.loop(exchange.send)
+
+    def pick(index, dst):
+        def body(at):
+            for j in range(64):
+                dst[pl.ds(at + j, 1), :] = wide[pl.ds(index[at + j], 1), :]
+
+        row_loop(count, 64, body)
+
+    pick(receivers, to_rows)
     w = w_in[0]
-    premultiply(nodes, w[LANES : 2 * LANES, :], table_r)
-    premultiply(edges, w[2 * LANES :, :], msg)
-
-    def gather_near(at):
-        for j in range(32):
-            msg[pl.ds(at + j, 1), :] = msg[pl.ds(at + j, 1), :] + table_r[pl.ds(receivers[at + j], 1), :]
-
-    row_loop(count, 32, gather_near)
-    premultiply(nodes, w[0:LANES, :], table_s)
+
+    def known(at):
+        block = pl.ds(at, 512)
+        to_rows[block, :] = dot(to_rows[block, :].astype(BF16), w[LANES : 2 * LANES, :]) + dot(
+            edges[block, :], w[2 * LANES :, :]
+        )
+
     each = groups // pieces
 
     def ready(s):
@@ -497,27 +540,28 @@
         if s == 0:
             exchange.own().wait()
 
-    def base(k):
-        p = net.behind(k // net.per) + lax.rem(k, net.per)
-        return p
-
-    part = doms // (pieces + 1) if doms % (pieces + 1) == 0 else doms // (2 * pieces)
-
     def work(s):
-        first = s * part
-        gather_blocks(pool_send, base, wide, rows, own_nodes, (first, part if s < pieces else doms - first))
-
-    Relay(net, ghosts, (r0, r1), [doms // pieces] * pieces).run(ready, work)
-    for owner in range(4):
-        block = ghosts[owner].reshape(doms * size, LANES)
-        table_s[pl.ds(near + owner * doms * size, doms * size), :] = dot(block, w[0:LANES, :])
-
-    def gather_far(at):
-        for j in range(32):
-            msg[pl.ds(at + j, 1), :] = msg[pl.ds(at + j, 1), :] + table_s[pl.ds(senders[at + j], 1), :]
-
-    row_loop(count, 32, gather_far)
-    edge_mlp(msg, w_out[0], gain[0:1, :], out)
+        if s == 0:
+            row_loop(count // 2, 512, known)
+        if s == pieces:
+            row_loop(count // 2, 512, lambda at: known(count // 2 + at))
+
+    part = doms // pieces
+
+    def got(owner, s):
+        at = pl.multiple_of(near + owner * (doms * size) + s * part * size, 16)
+        block = ghosts[owner, pl.ds(s * part, part)].reshape(part * size, LANES)
+        wide[pl.ds(at, part * size), :] = block.astype(F32)
+
+    Relay(net, ghosts, (r0, r1), [part] * pieces).run(ready, work, got)
+    pick(senders, from_rows)
+
+    def finish(at):
+        block = pl.ds(at, 512)
+        pre = dot(from_rows[block, :].astype(BF16), w[0:LANES, :]) + to_rows[block, :]
+        out[block, :] = normed(dot(silu(pre).astype(BF16), w_out[0]), gain[0:1, :])
+
+    row_loop(count, 512, finish)
     exchange.loop(lambda t: exchange.each(t, lambda i: exchange.copy(t, i).wait_send()))
 
 
@@ -525,49 +569,42 @@
     return pltpu.CompilerParams(collective_id=collective_id, has_side_effects=True)
 
 
-def message_stage(doms, groups, halo, pool_send, senders, receivers, nodes, edges, w_in, w_out, gain, pieces=2):
-    size, own_size = halo.shape[1], pool_send.shape[1]
+def message_stage(doms, groups, halo, senders, receivers, nodes, edges, w_in, w_out, gain, pieces=2):
+    size = halo.shape[1]
     near, count = nodes.shape[0], edges.shape[0]
     return pl.pallas_call(
         functools.partial(message_kernel, groups, pieces),
-        out_shape=(
-            jax.ShapeDtypeStruct((count, LANES), F32),
-            jax.ShapeDtypeStruct((doms, own_size, LANES), BF16),
-        ),
-        in_specs=[SMEM] * 4 + [VMEM] * 5,
-        out_specs=(VMEM, VMEM),
+        out_shape=jax.ShapeDtypeStruct((count, LANES), F32),
+        in_specs=[SMEM] * 3 + [VMEM] * 5,
+        out_specs=VMEM,
         scratch_shapes=[
             pltpu.VMEM((4, doms, size, LANES), BF16),
-            pltpu.VMEM(nodes.shape, F32),
-            pltpu.VMEM((doms * own_size, LANES), F32),
+            pltpu.VMEM((near + 4 * doms * size, LANES), F32),
+            pltpu.VMEM((doms * size, LANES), F32),
             pltpu.VMEM((doms, size, LANES), BF16),
-            pltpu.VMEM((near + 4 * doms * size, LANES), F32),
-            pltpu.VMEM((near, LANES), F32),
+            pltpu.VMEM((count, LANES), F32),
             pltpu.VMEM((count, LANES), F32),
         ]
         + exchange_sems(doms)
         + relay_sems(pieces),
         compiler_params=comm_params(0),
         name="message_stage",
-    )(halo, pool_send, senders, receivers, nodes, edges, w_in, w_out, gain)
-
-
-def child_counts(all_dest, first, counts, step=128):
+    )(halo, senders, receivers, nodes, edges, w_in, w_out, gain)
+
+
+def child_counts(all_dest, first, counts, at, step):
     lines, width = all_dest.shape
 
-    def rows(at):
-        target = lax.broadcasted_iota(jnp.int32, (step, width), 0) + (first + at)
-
-        def line(i, total):
-            for j in range(4):
-                hit = all_dest[pl.ds(i * 4 + j, 1), :] == target
-                total = total + jnp.where(hit, 1.0, 0.0)
-            return total
-
-        total = lax.fori_loop(0, lines // 4, line, jnp.zeros((step, width), F32))
-        counts[pl.ds(at, step), :] = jnp.broadcast_to(jnp.sum(total, axis=1, keepdims=True), (step, LANES))
-
-    row_loop(counts.shape[0], step, rows)
+    target = lax.broadcasted_iota(jnp.int32, (step, width), 0) + (first + at)
+
+    def line(i, total):
+        for j in range(4):
+            hit = all_dest[pl.ds(i * 4 + j, 1), :] == target
+            total = total + jnp.where(hit, 1.0, 0.0)
+        return total
+
+    total = lax.fori_loop(0, lines // 4, line, jnp.zeros((step, width), F32))
+    counts[pl.ds(at, step), :] = jnp.broadcast_to(jnp.sum(total, axis=1, keepdims=True), (step, LANES))
 
 
 def one_hot(index, first, rows):
@@ -576,10 +613,10 @@
 
 
 def main_kernel(
-    groups, pieces, halo, dest, senders, receivers, place, all_dest, group_dest, line_receivers,
+    groups, pieces, halo, own, dest, senders, receivers, place, all_dest, group_dest, line_receivers,
     part_there, nodes_there, edges, edge_in, edge_out, node_in, node_out, edge_gain, node_gain,
     coarse_out, fine_out,
-    table, fine_wide, part, nodes, load_sems, hop, passed, near, mid, arrived, counts, pooled, coarse_part, coarse_hop, coarse_passed, coarse_near,
+    table, fine_wide, part, fine_nodes, nodes, load_sems, hop, passed, near, mid, arrived, counts, pooled, coarse_part, coarse_hop, coarse_passed, coarse_near,
     coarse_in, ghosts, wide, rows, border, table_s, table_r, msg, send, land,
     f0, f1, p0, p1, e0, e1, a0, a1, b0, b1, g0, g1, h0, h1, i0, i1, i2, j0, j1, j2, k0, k1, k2,
 ):
@@ -588,15 +625,20 @@
     coarse_rows, count = 4 * quarter, edges.shape[0]
     net = Net(doms, groups)
     load_part = pltpu.make_async_copy(part_there, part, load_sems.at[0])
-    load_nodes = pltpu.make_async_copy(nodes_there, nodes, load_sems.at[1])
+    load_nodes = pltpu.make_async_copy(nodes_there, fine_nodes, load_sems.at[1])
+    load_nodes.start()
     load_part.start()
-    load_nodes.start()
     net.greet()
     premultiply(edges, edge_in[1, 2 * LANES :, :], msg)
-    child_counts(all_dest, net.e * quarter, counts)
-    pooled[...] = jnp.zeros_like(pooled)
+    load_nodes.wait()
+    widen(fine_nodes, fine_wide)
+
+    def line(k):
+        return net.behind(k // net.per) + lax.rem(k, net.per)
+
+    half = doms // 2
+    gather_blocks(own, line, fine_wide, rows, nodes, (half, half))
     load_part.wait()
-    load_nodes.wait()
     net.meet()
 
     reduce = Reduce(net, part, hop, passed, near, (f0, f1), groups // 2)
@@ -610,7 +652,7 @@
     span = net.per * size
 
     def use(c):
-        units = (groups // 2 + c, c)
+        units = (2 * c + 1, 2 * c)
         for u in units:
             own = nodes[u * net.per : (u + 1) * net.per].reshape(span, LANES)
             result = node_mlp(own, reduce.value(pl.ds(u * span, span)), node_in[0], node_out[0], node_gain[0:1, :])
@@ -619,12 +661,17 @@
             pool.own().start()
         for u in units:
             pool.send(u)
-
-    reduce.run(use)
+        step = 2 * quarter // groups
+        child_counts(all_dest, net.e * quarter, counts, c * step, step)
+
+    def aside():
+        gather_blocks(own, line, fine_wide, rows, nodes, (0, half))
+        pooled[...] = jnp.zeros_like(pooled)
+
+    reduce.run(use, aside)
 
     def gathered(k, carry):
-        c = groups // 2 - 1 - k // 2
-        t = c + (1 - lax.rem(k, 2)) * (groups // 2)
+        t = groups - 1 - k
         pool.receive(t)
 
         @pl.when(t == 0)
@@ -647,16 +694,24 @@
 
     def spread(values):
         def got(owner, s):
-            wide[pl.ds(pl.multiple_of(owner * quarter, quarter), quarter), :] = values[owner].astype(F32)
+            at = pl.ds(pl.multiple_of(owner * quarter + s * share, share), share)
+            wide[at, :] = values[owner, s * share : (s + 1) * share].astype(F32)
 
         return got
 
     reduce = Reduce(net, coarse_part, coarse_hop, coarse_passed, coarse_near, (p0, p1), p0.shape[1])
-    reduce.run()
-    mean = reduce.value(pl.ds(0, quarter)) / jnp.maximum(counts[...], 1.0)
-    coarse_in[net.e] = mean.astype(BF16)
-    Relay(net, coarse_in, (g0, g1), [quarter]).run(got=spread(coarse_in))
-    gather_blocks(halo, lambda k: k, wide, rows, border, (0, doms))
+    chunks = p0.shape[1]
+    share = quarter // chunks
+    relay = Relay(net, coarse_in, (g0, g1), [share] * chunks)
+
+    def mean(c):
+        at = pl.ds(c * share, share)
+        coarse_in[net.e, at] = (reduce.value(at) / jnp.maximum(counts[at, :], 1.0)).astype(BF16)
+        relay.first(c)
+
+    reduce.run(mean)
+    relay.rest(spread(coarse_in))
+    gather_blocks(halo, lambda k: k, wide, rows, border, (0, doms), True)
     here = ghosts.at[net.e]
     exchange = Exchange(
         net, net.ahead,
@@ -708,12 +763,18 @@
         coarse_part[owner] = (sums[:, 0:LANES] + sums[:, LANES:]).astype(BF16)
 
     reduce = Reduce(net, coarse_part, coarse_hop, coarse_passed, coarse_near, (e0, e1), e0.shape[1])
-    reduce.run()
-    coarse_out[net.e] = node_mlp(
-        coarse_in[net.e], reduce.value(pl.ds(0, quarter)), node_in[1], node_out[1], node_gain[1:2, :]
-    )
     wide[pl.ds(coarse_rows, 8), :] = jnp.zeros((8, LANES), F32)
-    Relay(net, coarse_out, (a0, a1), [quarter]).run(got=spread(coarse_out))
+    relay_out = Relay(net, coarse_out, (a0, a1), [share] * chunks)
+
+    def updated(c):
+        at = pl.ds(c * share, share)
+        coarse_out[net.e, at] = node_mlp(
+            coarse_in[net.e, at], reduce.value(at), node_in[1], node_out[1], node_gain[1:2, :]
+        )
+        relay_out.first(c)
+
+    reduce.run(updated)
+    relay_out.rest(spread(coarse_out))
     back = Exchange(
         net, net.ahead,
         lambda t, peer: send.at[peer],
@@ -761,10 +822,12 @@
     back.loop(lambda t: back.each(t, lambda i: back.copy(t, i).wait_send()))
 
 
-def main_stage(groups, coarse_rows, ints, part, nodes, edges, weights, fine_rows, pieces=(2, 2, 2, 1, 1)):
-    doms, size, _ = nodes.shape
+def main_stage(groups, coarse_rows, ints, part, fine_nodes, edges, weights, pieces=(2, 2, 2, 1, 1)):
+    doms, size = ints[1].shape
+    fine_rows = fine_nodes.shape[0]
+    nodes = jax.ShapeDtypeStruct((doms, size, LANES), BF16)
     quarter = coarse_rows // 4
-    border_size, count = ints[0].shape[1], edges.shape[0]
+    border_size, count = ints[0].shape[0], edges.shape[0]
     vmem = pltpu.VMEM
     return pl.pallas_call(
         functools.partial(main_kernel, groups, pieces),
@@ -772,12 +835,13 @@
             jax.ShapeDtypeStruct((4, quarter, LANES), BF16),
             jax.ShapeDtypeStruct((fine_rows, LANES), BF16),
         ),
-        in_specs=[SMEM] * 5 + [VMEM] * 3 + [ANY] * 2 + [VMEM] * 7,
+        in_specs=[SMEM] * 6 + [VMEM] * 3 + [ANY] * 2 + [VMEM] * 7,
         out_specs=(VMEM, VMEM),
         scratch_shapes=[
             vmem((4,) + nodes.shape, BF16),
             vmem((4 * doms * size, LANES), F32),
             vmem(part.shape, BF16),
+            vmem(fine_nodes.shape, BF16),
             vmem(nodes.shape, BF16),
             pltpu.SemaphoreType.DMA((2,)),
         ]
@@ -805,16 +869,16 @@
         + reduce_scratch(quarter, groups // 2)[3:]
         + reduce_scratch(quarter, 2)[3:]
         + reduce_scratch(quarter, 2)[3:]
-        + relay_sems(1)
+        + relay_sems(2)
         + relay_sems(len(pieces))
-        + relay_sems(1)
+        + relay_sems(2)
         + relay_sems(2)
         + exchange_sems(doms)
         + exchange_sems(doms)
         + exchange_sems(doms),
         compiler_params=comm_params(1),
         name="main_stage",
-    )(*ints, part, nodes, edges, *weights)
+    )(*ints, part, fine_nodes, edges, *weights)
 
 
 def shards(groups, coarse_rows, *args):
@@ -824,31 +888,25 @@
         pool_send, pool_dest, unpool_slot,
         edge_in_weight, edge_out_weight, node_in_weight, node_out_weight, edge_gain, node_gain,
     ) = args
-    e = lax.axis_index("edge")
     doms = fine_halo.shape[1]
     slots = pool_dest.shape[2]
-
-    def quarter(lists):
-        size = lists.shape[2] // 4
-        return lax.dynamic_slice_in_dim(lists[0], e * size, size, axis=1)
-
-    own, dest = quarter(pool_send), quarter(pool_dest)
-    group_dest = dest.reshape(groups, -1)
     widths = (doms, fine_nodes.shape[0], fine_halo.shape[2], coarse_rows, coarse_halo.shape[2], slots)
-    senders, far_senders, place = place_stage(groups, widths, fine_senders, coarse_senders, unpool_slot)
-
-    msg, own_nodes = message_stage(
-        doms, groups, quarter(fine_halo), own, senders, fine_receivers,
+    senders, far_senders, place, border, own, dest, far_border = place_stage(
+        groups, widths, (fine_senders, coarse_senders, unpool_slot),
+        ((fine_halo[0], 1), (pool_send[0], 1), (pool_dest[0], 1), (coarse_halo[0].T, 0)),
+    )
+    msg = message_stage(
+        doms, groups, border, senders, fine_receivers,
         fine_nodes, fine_edges, edge_in_weight, edge_out_weight, edge_gain,
     )
     part = sum_stage(fine_receivers, place, msg, doms * slots)
     ints = (
-        quarter(coarse_halo), dest, far_senders, coarse_receivers, place,
-        pool_dest[0], group_dest, coarse_receivers.reshape(1, -1),
+        far_border, own, dest, far_senders, coarse_receivers, place,
+        pool_dest[0], dest.reshape(groups, -1), coarse_receivers.reshape(1, -1),
     )
     weights = (edge_in_weight, edge_out_weight, node_in_weight, node_out_weight, edge_gain, node_gain)
     coarse_out, fine_out = main_stage(
-        groups, coarse_rows, ints, part.reshape(4, -1, LANES), own_nodes, coarse_edges, weights, fine_nodes.shape[0]
+        groups, coarse_rows, ints, part.reshape(4, -1, LANES), fine_nodes, coarse_edges, weights
     )
     return fine_out, coarse_out.reshape(-1, LANES)
 

time: 231 us -> 217 us (0.939)
  Pallas kernels: 219 us -> 210 us
  local copies, waits for them, and re-layouts: 10.6 us -> 5.33 us
    pallas_call x1, Pallas kernels: 48.3 us -> 40.9 us  [message_stage(): pl.pallas_call(functools.partial(message_kernel, groups, pieces), out_sha...]
    dynamic_slice x6 -> x0, local copies, waits for them, and re-layouts: 6.01 us -> none  [quarter(): return lax.dynamic_slice_in_dim(lists[0], e * size, size, axis=1)]
where the time goes in v4:
time: 217 us; the launch traced here: 216 us
  Pallas kernels  210 us (97%)
  local copies, waits for them, and re-layouts  5.33 us (2%)
    pallas_call x1, Pallas kernels, main_stage(): pl.pallas_call(functools.partial(main_kernel, groups, pieces), out_shape=...  155 us
    pallas_call x1, Pallas kernels, message_stage(): pl.pallas_call(functools.partial(message_kernel, groups, pieces), out_sha...  40.9 us
    pallas_call x1, Pallas kernels, sum_stage(): pl.pallas_call(sum_kernel, out_shape=jax.ShapeDtypeStruct((slots, LANES),...  12.3 us

profile of v4, /device:TPU:1, one launch (start us, length us, event | category | flops | bytes accessed | tf_op | source)
XLA Modules:
  0.0 215.6 jit_solution(14441123883814356607)
XLA Ops:
  0.6 1.9 place_stage.1
  2.5 1.4 reshape.39.group_dest
  4.0 40.9 %message_stage.1.msg = f32[4096,128]{1,0:T(8,128)} custom-call(s32[64,16]{1,0:T(8,128)} %get-tuple-element.16.halo, s32[4096]{0:T(1024)} %bitcast.24, s32[4096]{0:T(1024)} %receivers.4, bf16[8192,128]{1,0:T(8,128)(2,1)} %nodes_there.1, bf16[4096,128]{1,0:T(8,128)(2,1)} %edges.2, bf16[2,384,128]{2,1,0:T(8,128)(2,1)} %edge_in.1, ...), custom_call_target="tpu_custom_call" | custom-call | tf_op jit(solution)/shard_map/message_stage/pallas_call | solution.py:575
  44.8 12.3 %sum_stage.1 = bf16[12288,128]{1,0:T(8,128)(2,1)} custom-call(s32[4096]{0:T(1024)} %receivers.4, s32[8192]{0:T(1024)} %bitcast.19, f32[4096,128]{1,0:T(8,128)} %message_stage.1.msg), custom_call_target="tpu_custom_call" | custom-call | tf_op jit(solution)/shard_map/sum_stage/pallas_call | solution.py:115
  57.1 154.6 %main_stage.1 = (bf16[4,512,128]{2,1,0:T(8,128)(2,1)}, bf16[8192,128]{1,0:T(8,128)(2,1)}) custom-call(s32[8,64]{1,0:T(8,128)} %get-tuple-element.11.halo, s32[64,48]{1,0:T(8,128)} %get-tuple-element.12.own, s32[64,48]{1,0:T(8,128)} %get-tuple-element.13.dest, s32[1024]{0:T(1024)} %bitcast.29, s32[1024]{0:T(1024)} %receivers.5, s32[8192]{0:T(1024)} %bitcast.20, ...), custom_call_target="tpu_custom_call" | custom-call | tf_op jit(solution)/shard_map/main_stage/pallas_call | solution.py:832
  211.7 0.0 copy-start
  211.7 3.1 %copy.22 = bf16[8192,128]{1,0:T(8,128)(2,1)} copy(bf16[8192,128]{1,0:T(8,128)(2,1)} %get-tuple-element.22) | data formatting | bytes 4194304
  214.8 0.0 copy-done
  214.8 0.8 copy.23
Async XLA Ops:
  211.7 3.1 %copy-start = (bf16[4,512,128]{2,1,0:T(8,128)(2,1)S(1)}, bf16[4,512,128]{2,1,0:T(8,128)(2,1)}, u32[]{:S(2)}) copy-start(bf16[4,512,128]{2,1,0:T(8,128)(2,1)} %get-tuple-element.19) | copy-start | bytes 1572868

commit v5 on v4

--- a/solution.py
+++ b/solution.py
@@ -106,7 +106,9 @@
     for q in range(4):
         at = pl.ds(q * size, size)
         sum_accs([acc.at[at] for acc in accs], total.at[at])
-        store(q).start()
+        if q:
+            store(q - 1).start()
+    store(3).start()
     for q in range(4):
         store(q).wait()
 
@@ -128,7 +130,7 @@
     )(receivers, place, msg)
 
 
-def place_kernel(groups, widths, senders, far_senders, slots, lists, out, far_out, place, cuts):
+def place_kernel(groups, widths, senders, far_senders, slots, lists, out, far_out, place, lined, cuts):
     me = lax.axis_index("dom")
     doms, rows, width, coarse_rows, coarse_width, slot_count = widths
     per = doms // groups
@@ -175,6 +177,8 @@
         for q in range(3):
             value = jnp.where(e == q, pieces[q], value)
         cut[...] = value
+    dest = cuts[2]
+    lined[...] = jnp.concatenate([dest[pl.ds(l, groups, stride=per), :] for l in range(per)], axis=1)
 
 
 def place_stage(groups, widths, ints, lists):
@@ -182,16 +186,17 @@
     cut_shapes = [
         tuple(n // 4 if i == axis else n for i, n in enumerate(whole.shape)) for whole, axis in lists
     ]
-    shapes = [x.shape for x in shaped] + cut_shapes
+    rows, size = cut_shapes[2]
+    shapes = [x.shape for x in shaped] + [(groups, rows // groups * size)] + cut_shapes
 
     def kernel(*refs):
         k = 3 + len(lists)
-        place_kernel(groups, widths, *refs[0:3], refs[3:k], *refs[k : k + 3], refs[k + 3 :])
+        place_kernel(groups, widths, *refs[0:3], refs[3:k], *refs[k : k + 4], refs[k + 4 :])
 
     results = pl.pallas_call(
         kernel,
         out_shape=[jax.ShapeDtypeStruct(s, jnp.int32) for s in shapes],
-        in_specs=[VMEM] * len(shapes),
+        in_specs=[VMEM] * (3 + len(lists)),
         out_specs=[VMEM] * len(shapes),
         name="place_stage",
     )(*shaped, *(whole for whole, _ in lists))
@@ -492,15 +497,18 @@
 
 
 def message_kernel(
-    groups, pieces, halo, senders, receivers, nodes, edges, w_in, w_out, gain,
-    out, ghosts, wide, rows, send, from_rows, to_rows, s0, s1, s2, r0, r1,
+    groups, pieces, halo, senders, receivers, nodes, edges_there, w_in, w_out, gain,
+    out, edges, load_sem, out_sem, ghosts, wide, rows, send, from_rows, to_rows, s0, s1, s2, r0, r1,
 ):
     doms, size = ghosts.shape[1], ghosts.shape[2]
     count, near = edges.shape[0], nodes.shape[0]
     net = Net(doms, groups)
+    load = pltpu.make_async_copy(edges_there, edges, load_sem)
+    load.start()
     net.greet()
     widen(nodes, wide)
     gather_blocks(halo, lambda k: k, wide, rows, send, (0, doms))
+    load.wait()
     net.meet()
     land = ghosts.at[net.e]
     exchange = Exchange(
@@ -556,12 +564,22 @@
     Relay(net, ghosts, (r0, r1), [part] * pieces).run(ready, work, got)
     pick(senders, from_rows)
 
+    def store(k):
+        block = pl.ds(pl.multiple_of(k * 512, 512), 512)
+        return pltpu.make_async_copy(from_rows.at[block], out.at[block], out_sem.at[k])
+
     def finish(at):
         block = pl.ds(at, 512)
         pre = dot(from_rows[block, :].astype(BF16), w[0:LANES, :]) + to_rows[block, :]
-        out[block, :] = normed(dot(silu(pre).astype(BF16), w_out[0]), gain[0:1, :])
+        from_rows[block, :] = normed(dot(silu(pre).astype(BF16), w_out[0]), gain[0:1, :])
+
+        @pl.when(at > 0)
+        def _():
+            store(at // 512 - 1).start()
 
     row_loop(count, 512, finish)
+    store(count // 512 - 1).start()
+    row_loop(count, 512, lambda at: store(at // 512).wait())
     exchange.loop(lambda t: exchange.each(t, lambda i: exchange.copy(t, i).wait_send()))
 
 
@@ -575,9 +593,12 @@
     return pl.pallas_call(
         functools.partial(message_kernel, groups, pieces),
         out_shape=jax.ShapeDtypeStruct((count, LANES), F32),
-        in_specs=[SMEM] * 3 + [VMEM] * 5,
-        out_specs=VMEM,
+        in_specs=[SMEM] * 3 + [VMEM, ANY] + [VMEM] * 3,
+        out_specs=ANY,
         scratch_shapes=[
+            pltpu.VMEM(edges.shape, BF16),
+            pltpu.SemaphoreType.DMA,
+            pltpu.SemaphoreType.DMA((count // 512,)),
             pltpu.VMEM((4, doms, size, LANES), BF16),
             pltpu.VMEM((near + 4 * doms * size, LANES), F32),
             pltpu.VMEM((doms * size, LANES), F32),
@@ -891,7 +912,7 @@
     doms = fine_halo.shape[1]
     slots = pool_dest.shape[2]
     widths = (doms, fine_nodes.shape[0], fine_halo.shape[2], coarse_rows, coarse_halo.shape[2], slots)
-    senders, far_senders, place, border, own, dest, far_border = place_stage(
+    senders, far_senders, place, group_dest, border, own, dest, far_border = place_stage(
         groups, widths, (fine_senders, coarse_senders, unpool_slot),
         ((fine_halo[0], 1), (pool_send[0], 1), (pool_dest[0], 1), (coarse_halo[0].T, 0)),
     )
@@ -902,7 +923,7 @@
     part = sum_stage(fine_receivers, place, msg, doms * slots)
     ints = (
         far_border, own, dest, far_senders, coarse_receivers, place,
-        pool_dest[0], dest.reshape(groups, -1), coarse_receivers.reshape(1, -1),
+        pool_dest[0], group_dest, coarse_receivers.reshape(1, -1),
     )
     weights = (edge_in_weight, edge_out_weight, node_in_weight, node_out_weight, edge_gain, node_gain)
     coarse_out, fine_out = main_stage(

time: 217 us -> 216 us (level)
  no operation moved by 1% of the time
where the time goes in v5:
time: 216 us; the launch traced here: 214 us
  Pallas kernels  209 us (97%)
  local copies, waits for them, and re-layouts  3.9 us (2%)
    pallas_call x1, Pallas kernels, main_stage(): pl.pallas_call(functools.partial(main_kernel, groups, pieces), out_shape=...  155 us
    pallas_call x1, Pallas kernels, message_stage(): pl.pallas_call(functools.partial(message_kernel, groups, pieces), out_sha...  40.4 us
    pallas_call x1, Pallas kernels, sum_stage(): pl.pallas_call(sum_kernel, out_shape=jax.ShapeDtypeStruct((slots, LANES),...  12.6 us

profile of v5, /device:TPU:1, one launch (start us, length us, event | category | flops | bytes accessed | tf_op | source)
XLA Modules:
  0.0 214.0 jit_solution(10367311711029767072)
XLA Ops:
  0.6 1.9 place_stage.1
  2.6 40.4 %message_stage.1.msg = f32[4096,128]{1,0:T(8,128)} custom-call(s32[64,16]{1,0:T(8,128)} %get-tuple-element.18.halo, s32[4096]{0:T(1024)} %bitcast.24, s32[4096]{0:T(1024)} %receivers.4, bf16[8192,128]{1,0:T(8,128)(2,1)} %nodes_there.1, bf16[4096,128]{1,0:T(8,128)(2,1)} %edges_there.1, bf16[2,384,128]{2,1,0:T(8,128)(2,1)} %edge_in.1, ...), custom_call_target="tpu_custom_call" | custom-call | tf_op jit(solution)/shard_map/message_stage/pallas_call | solution.py:593
  42.9 12.6 %sum_stage.1 = bf16[12288,128]{1,0:T(8,128)(2,1)} custom-call(s32[4096]{0:T(1024)} %receivers.4, s32[8192]{0:T(1024)} %bitcast.19, f32[4096,128]{1,0:T(8,128)} %message_stage.1.msg), custom_call_target="tpu_custom_call" | custom-call | tf_op jit(solution)/shard_map/sum_stage/pallas_call | solution.py:117
  55.5 154.6 %main_stage.1 = (bf16[4,512,128]{2,1,0:T(8,128)(2,1)}, bf16[8192,128]{1,0:T(8,128)(2,1)}) custom-call(s32[8,64]{1,0:T(8,128)} %get-tuple-element.12.halo, s32[64,48]{1,0:T(8,128)} %get-tuple-element.13.own, s32[64,48]{1,0:T(8,128)} %get-tuple-element.14.dest, s32[1024]{0:T(1024)} %bitcast.29, s32[1024]{0:T(1024)} %receivers.5, s32[8192]{0:T(1024)} %bitcast.20, ...), custom_call_target="tpu_custom_call" | custom-call | tf_op jit(solution)/shard_map/main_stage/pallas_call | solution.py:853
  210.1 0.0 copy-start
  210.1 3.1 %copy.22 = bf16[8192,128]{1,0:T(8,128)(2,1)} copy(bf16[8192,128]{1,0:T(8,128)(2,1)} %get-tuple-element.24) | data formatting | bytes 4194304
  213.2 0.0 copy-done
  213.3 0.8 copy.23
Async XLA Ops:
  210.1 3.1 %copy-start = (bf16[4,512,128]{2,1,0:T(8,128)(2,1)S(1)}, bf16[4,512,128]{2,1,0:T(8,128)(2,1)}, u32[]{:S(2)}) copy-start(bf16[4,512,128]{2,1,0:T(8,128)(2,1)} %get-tuple-element.21) | copy-start | bytes 1572868

commit v6 on v5

--- a/solution.py
+++ b/solution.py
@@ -57,7 +57,7 @@
     row_loop(accs[0].shape[0] // step * step, step, body)
 
 
-def add_rows(where, values, count, accs, unroll=32):
+def add_rows(where, values, count, accs, unroll=64):
     def body(at):
         for j in range(unroll):
             acc, row = accs[j % len(accs)], where(at + j)
@@ -125,7 +125,7 @@
             pltpu.SemaphoreType.DMA,
             pltpu.SemaphoreType.DMA((4,)),
         ]
-        + [pltpu.VMEM((slots, LANES), F32)] * 3,
+        + [pltpu.VMEM((slots, LANES), F32)] * 4,
         name="sum_stage",
     )(receivers, place, msg)
 

time: 216 us -> 214 us (level)
  no operation moved by 1% of the time
where the time goes in v6:
time: 214 us
  Pallas kernels  209 us (98%)
  local copies, waits for them, and re-layouts  3.9 us (2%)
    pallas_call x1, Pallas kernels, main_stage(): pl.pallas_call(functools.partial(main_kernel, groups, pieces), out_shape=...  156 us
    pallas_call x1, Pallas kernels, message_stage(): pl.pallas_call(functools.partial(message_kernel, groups, pieces), out_sha...  40.4 us
    pallas_call x1, Pallas kernels, sum_stage(): pl.pallas_call(sum_kernel, out_shape=jax.ShapeDtypeStruct((slots, LANES),...  11.2 us

profile of v6, /device:TPU:1, one launch (start us, length us, event | category | flops | bytes accessed | tf_op | source)
XLA Modules:
  0.0 213.8 jit_solution(10565052137391071580)
XLA Ops:
  0.6 1.9 place_stage.1
  2.6 40.4 %message_stage.1.msg = f32[4096,128]{1,0:T(8,128)} custom-call(s32[64,16]{1,0:T(8,128)} %get-tuple-element.18.halo, s32[4096]{0:T(1024)} %bitcast.24, s32[4096]{0:T(1024)} %receivers.4, bf16[8192,128]{1,0:T(8,128)(2,1)} %nodes_there.1, bf16[4096,128]{1,0:T(8,128)(2,1)} %edges_there.1, bf16[2,384,128]{2,1,0:T(8,128)(2,1)} %edge_in.1, ...), custom_call_target="tpu_custom_call" | custom-call | tf_op jit(solution)/shard_map/message_stage/pallas_call | solution.py:593
  42.9 11.2 %sum_stage.1 = bf16[12288,128]{1,0:T(8,128)(2,1)} custom-call(s32[4096]{0:T(1024)} %receivers.4, s32[8192]{0:T(1024)} %bitcast.19, f32[4096,128]{1,0:T(8,128)} %message_stage.1.msg), custom_call_target="tpu_custom_call" | custom-call | tf_op jit(solution)/shard_map/sum_stage/pallas_call | solution.py:117
  54.2 155.7 %main_stage.1 = (bf16[4,512,128]{2,1,0:T(8,128)(2,1)}, bf16[8192,128]{1,0:T(8,128)(2,1)}) custom-call(s32[8,64]{1,0:T(8,128)} %get-tuple-element.12.halo, s32[64,48]{1,0:T(8,128)} %get-tuple-element.13.own, s32[64,48]{1,0:T(8,128)} %get-tuple-element.14.dest, s32[1024]{0:T(1024)} %bitcast.29, s32[1024]{0:T(1024)} %receivers.5, s32[8192]{0:T(1024)} %bitcast.20, ...), custom_call_target="tpu_custom_call" | custom-call | tf_op jit(solution)/shard_map/main_stage/pallas_call | solution.py:853
  209.9 0.0 copy-start
  209.9 3.1 %copy.22 = bf16[8192,128]{1,0:T(8,128)(2,1)} copy(bf16[8192,128]{1,0:T(8,128)(2,1)} %get-tuple-element.24) | data formatting | bytes 4194304
  213.0 0.0 copy-done
  213.0 0.8 copy.23
Async XLA Ops:
  209.9 3.1 %copy-start = (bf16[4,512,128]{2,1,0:T(8,128)(2,1)S(1)}, bf16[4,512,128]{2,1,0:T(8,128)(2,1)}, u32[]{:S(2)}) copy-start(bf16[4,512,128]{2,1,0:T(8,128)(2,1)} %get-tuple-element.21) | copy-start | bytes 1572868
